TPU v7x, 128 devices: a whole 4x4x4 slice. The times are simulated.
128 devices in a mesh: tp: 4 (over x), ep: 32 (over z, y, core).
Axes of the slice: x: 4, y: 4, z: 4, core: 2. Of those that a mesh axis runs over, the one named last changes fastest.
Arguments:
- tokens: bfloat16 [4096, 5120], P('ep', 'tp'), may hold values from -6 to 6
- cotangent: bfloat16 [4096, 5120], P('ep', 'tp'), may hold values from -6 to 6
- expert_ids: int32 [4096, 3], P('ep'), may hold values from 0 to 31, all different within a row; in each aligned block of 128 rows (0 to 127, 128 to 255, ...) at most 15 rows name the same one
- gate_weights: float32 [4096, 4], P('ep'), may hold values from 0.1 to 1
- shadow_mask: int32 [4096], P('ep'), may hold values 0 or 1
- w_gate: bfloat16 [32, 5120, 1536], P('ep', None, 'tp'), may hold values from -0.078125 to 0.078125
- w_up: bfloat16 [32, 5120, 1536], P('ep', None, 'tp'), may hold values from -0.078125 to 0.078125
- w_down: bfloat16 [32, 1536, 5120], P('ep', 'tp'), may hold values from -0.15625 to 0.15625
- s_gate: bfloat16 [5120, 1536], P('ep', 'tp'), may hold values from -0.078125 to 0.078125
- s_up: bfloat16 [5120, 1536], P('ep', 'tp'), may hold values from -0.078125 to 0.078125
- s_down: bfloat16 [1536, 5120], P('tp', 'ep'), may hold values from -0.15625 to 0.15625
Outputs:
- mixed: bfloat16 [4096, 5120], P('ep', 'tp')
- grad_gate: bfloat16 [32, 5120, 1536], P('ep', None, 'tp')
- grad_up: bfloat16 [32, 5120, 1536], P('ep', None, 'tp')
- grad_down: bfloat16 [32, 1536, 5120], P('ep', 'tp')
- grad_s_gate: bfloat16 [5120, 1536], P('ep', 'tp')
- grad_s_up: bfloat16 [5120, 1536], P('ep', 'tp')
- grad_s_down: bfloat16 [1536, 5120], P('tp', 'ep')
Inputs may be any that keep to these rules, and one draw needn't show every extreme that they name: `expert_ids`: each row names 3 different experts. Among the 128 rows of one device no expert is named more than 15 times, and in every draw some expert is named exactly 15 times by the rows of some device.
All inputs are finite; a program needn't handle non-finite values. No bound on the sum of `shadow_mask` on one device may be relied on, other than what follows from the above.
Results may differ from a plain program's by a relative error of at most 0.028.
Values may be sent and summed in bfloat16 or wider, within the bound.
A program may use at most 192 MiB of HBM per device.

v0:
```python
import jax
import jax.numpy as jnp
from jax import lax
from jax.sharding import PartitionSpec as P


def sent_together(arrays, axis, dim, along):
    widths = [a.shape[along] for a in arrays]
    both = jnp.concatenate(arrays, axis=along)
    whole = lax.all_gather(both, axis, axis=dim, tiled=True)
    return tuple(jnp.split(whole, [sum(widths[:k]) for k in range(1, len(widths))], axis=along))


def turned_gather(arrays, axis, dims):
    turned = [jnp.moveaxis(a, dim, 0) for a, dim in zip(arrays, dims)]
    both = jnp.concatenate([t.reshape(len(t), -1) for t in turned], axis=1)
    whole, at, outs = (lax.all_gather(both, axis, axis=0, tiled=True), 0, [])
    for t, dim in zip(turned, dims):
        share = whole[:, at : at + t[0].size].reshape(-1, *t.shape[1:])
        outs.append(jnp.moveaxis(share, 0, dim))
        at += t[0].size
    return tuple(outs)


def sent_together_2(arrays, axis, dim, along):
    widths = [a.shape[along] for a in arrays]
    both = jnp.concatenate(arrays, axis=along)
    whole = lax.psum_scatter(both, axis, scatter_dimension=dim, tiled=True)
    return tuple(jnp.split(whole, [sum(widths[:k]) for k in range(1, len(widths))], axis=along))


def contract_rows(left, right):
    return lax.dot_general(
        left, right, (((0,), (0,)), ((), ())), preferred_element_type=jnp.float32
    )


def split_parts(values):
    upper_part = values.astype(jnp.bfloat16)
    lower_part = (values - upper_part.astype(jnp.float32)).astype(jnp.bfloat16)
    return (upper_part, lower_part)


def weigh_rows(weight_table, rows):
    weight_upper, weight_lower = split_parts(weight_table)
    if rows.dtype == jnp.bfloat16:
        return jnp.dot(weight_upper, rows, preferred_element_type=jnp.float32) + jnp.dot(
            weight_lower, rows, preferred_element_type=jnp.float32
        )
    rows_upper, rows_lower = split_parts(rows)
    return (
        jnp.dot(weight_upper, rows_upper, preferred_element_type=jnp.float32)
        + jnp.dot(weight_upper, rows_lower, preferred_element_type=jnp.float32)
        + jnp.dot(weight_lower, rows_upper, preferred_element_type=jnp.float32)
    )


def expert_pass(rows_x, rows_dout, weight_gate, weight_up, weight_down):
    pre_gate = jnp.dot(rows_x, weight_gate, preferred_element_type=jnp.float32)
    pre_up = jnp.dot(rows_x, weight_up, preferred_element_type=jnp.float32)
    sigmoid_gate = jax.nn.sigmoid(pre_gate)
    activated = pre_gate * sigmoid_gate
    hidden = (activated * pre_up).astype(jnp.bfloat16)
    partial_out = jnp.dot(hidden, weight_down, preferred_element_type=jnp.float32).astype(
        jnp.bfloat16
    )
    hidden_grad = lax.dot_general(
        rows_dout, weight_down, (((1,), (1,)), ((), ())), preferred_element_type=jnp.float32
    )
    grad_pre_gate = (
        hidden_grad * pre_up * sigmoid_gate * (1.0 + pre_gate * (1.0 - sigmoid_gate))
    ).astype(jnp.bfloat16)
    grad_pre_up = (hidden_grad * activated).astype(jnp.bfloat16)
    return (partial_out, hidden, grad_pre_gate, grad_pre_up)


def shards(
    tokens,
    cotangent,
    expert_ids,
    gate_weights,
    shadow_mask,
    w_gate,
    w_up,
    w_down,
    s_gate,
    s_up,
    s_down,
):
    ep_count = lax.axis_size("ep")
    tok_count, top_count = expert_ids.shape
    quarter_width = tokens.shape[1]
    width = quarter_width * lax.axis_size("tp")
    expert_count = w_gate.shape[0] * ep_count
    capacity = (5 * tok_count * top_count + 4 * expert_count - 1) // (4 * expert_count)
    slot_count = expert_count * capacity
    picks_flat = expert_ids.reshape(-1)
    onehot = (picks_flat[:, None] == jnp.arange(expert_count, dtype=jnp.int32)[None, :]).astype(
        jnp.int32
    )
    slot_rank = jnp.sum((jnp.cumsum(onehot, axis=0) - onehot) * onehot, axis=1)
    slot_index = (picks_flat * capacity + slot_rank).reshape(tok_count, top_count)
    matches = jnp.arange(slot_count, dtype=jnp.int32)[:, None, None] == slot_index[None, :, :]
    dispatch = jnp.any(matches, axis=2).astype(jnp.bfloat16)
    weighting = jnp.sum(jnp.where(matches, gate_weights[None, :, :top_count], 0.0), axis=2)
    slot_gate = jnp.sum(weighting, axis=1)
    shadow_weight = gate_weights[:, top_count] * shadow_mask.astype(jnp.float32)
    x_full, dy_full = sent_together((tokens, cotangent), "tp", 1, 0)
    rows_x = jnp.dot(dispatch, x_full, preferred_element_type=jnp.float32).astype(jnp.bfloat16)
    rows_dy = jnp.dot(dispatch, dy_full, preferred_element_type=jnp.float32)
    rows_dout = (slot_gate[:, None] * rows_dy).astype(jnp.bfloat16)
    recv_x, recv_dout = (
        lax.all_to_all(
            rows_x.reshape(ep_count, -1, width), "ep", split_axis=0, concat_axis=0, tiled=True
        ),
        lax.all_to_all(
            rows_dout.reshape(ep_count, -1, width), "ep", split_axis=0, concat_axis=0, tiled=True
        ),
    )
    expert_x = recv_x.reshape(-1, width)
    expert_dout = recv_dout.reshape(-1, width)
    partial_out, hidden, grad_pre_gate, grad_pre_up = expert_pass(
        expert_x, expert_dout, w_gate[0], w_up[0], w_down[0]
    )
    grad_gate = contract_rows(expert_x, grad_pre_gate).astype(jnp.bfloat16)[None]
    grad_up = contract_rows(expert_x, grad_pre_up).astype(jnp.bfloat16)[None]
    grad_down = contract_rows(hidden, expert_dout).astype(jnp.bfloat16)[None]
    full_gate, full_up, full_down = turned_gather((s_gate, s_up, s_down), "ep", (0, 0, 1))
    shadow_dout = (shadow_weight[:, None] * dy_full.astype(jnp.float32)).astype(jnp.bfloat16)
    shadow_out, shadow_hidden, shadow_gate_pre, shadow_up_pre = expert_pass(
        x_full, shadow_dout, full_gate, full_up, full_down
    )
    shadow_sums = lax.psum_scatter(
        jnp.concatenate(
            [
                contract_rows(x_full, shadow_gate_pre),
                contract_rows(x_full, shadow_up_pre),
                contract_rows(shadow_dout, shadow_hidden),
            ],
            axis=1,
        ).astype(jnp.bfloat16),
        "ep",
        scatter_dimension=0,
        tiled=True,
    ).astype(jnp.float32)
    hidden_part = s_gate.shape[1]
    grad_s_gate = shadow_sums[:, :hidden_part].astype(jnp.bfloat16)
    grad_s_up = shadow_sums[:, hidden_part : 2 * hidden_part].astype(jnp.bfloat16)
    grad_s_down = shadow_sums[:, 2 * hidden_part :].T.astype(jnp.bfloat16)
    expert_sum, shadow_sum = tuple(
        (
            part.astype(jnp.float32)
            for part in sent_together_2((partial_out, shadow_out), "tp", 1, 0)
        )
    )
    back_sums = (
        lax.all_to_all(
            expert_sum.reshape(ep_count, -1, quarter_width).astype(jnp.bfloat16),
            "ep",
            split_axis=0,
            concat_axis=0,
            tiled=True,
        )
        .astype(jnp.float32)
        .reshape(-1, quarter_width)
    )
    combined = weigh_rows(weighting.T, back_sums)
    mixed = (combined + shadow_weight[:, None] * shadow_sum).astype(jnp.bfloat16)
    return (mixed, grad_gate, grad_up, grad_down, grad_s_gate, grad_s_up, grad_s_down)


def solution(mesh):
    return jax.shard_map(
        shards,
        mesh=mesh,
        in_specs=(
            P("ep", "tp"),
            P("ep", "tp"),
            P("ep", None),
            P("ep", None),
            P("ep"),
            P("ep", None, "tp"),
            P("ep", None, "tp"),
            P("ep", "tp", None),
            P("ep", "tp"),
            P("ep", "tp"),
            P("tp", "ep"),
        ),
        out_specs=(
            P("ep", "tp"),
            P("ep", None, "tp"),
            P("ep", None, "tp"),
            P("ep", "tp", None),
            P("ep", "tp"),
            P("ep", "tp"),
            P("tp", "ep"),
        ),
        check_vma=False,
    )
```

profile of v0, /device:TPU:1, one launch (start us, length us, event | category | flops | bytes accessed | tf_op | source)
XLA Modules:
  0.0 355.0 jit_solution(1410645088929357484)
XLA Ops:
  7.2 2.0 pad_maximum_fusion.2
  9.2 1.8 pad_maximum_fusion.3
  11.1 0.8 copy.50
  11.9 0.2 eq.43
  12.1 0.2 eq.39
  12.3 0.9 reduce-window.6
  13.2 0.2 slice_reduce_fusion
  13.8 0.7 multiply_add_fusion
  14.6 33.7 %all-gather.3.cloned.1.call-done = bf16[256,5120]{1,0:T(8,128)(2,1)} async-done(((bf16[256,1280]{1,0:T(8,128)(2,1)}), bf16[256,5120]{1,0:T(8,128)(2,1)}) %all-gather.3.cloned.1.call-update) | async-done | bytes 2621456 | tf_op jit(solution)/shard_map/all_gather | solution.py:10
  48.4 4.9 %convolution_convert_fusion = bf16[480,5120]{1,0:T(8,128)(2,1)} fusion(pred[480,128]{1,0:T(8,128)(4,1)S(1)} %fusion.21, bf16[256,5120]{1,0:T(8,128)(2,1)} %all-gather.3.cloned.1.call-done), kind=kOutput, calls=%fused_computation.2 | convolution fusion | flops 631603200 | bytes 6287360 | tf_op jit(solution)/shard_map/dot_general | solution.py:109
  53.3 5.8 %reshape.62 = bf16[32,15,5120]{2,1,0:T(8,128)(2,1)} reshape(bf16[480,5120]{1,0:T(8,128)(2,1)} %convolution_convert_fusion) | data formatting | bytes 9830400 | tf_op jit(solution)/shard_map/reshape | solution.py:114
  59.1 80.9 %all_to_all.15 = bf16[32,15,5120]{2,1,0:T(8,128)(2,1)} all-to-all(bf16[32,15,5120]{2,1,0:T(8,128)(2,1)} %reshape.62), channel_id=1, replica_groups=mesh['tp'=4,'ep'=32] {'ep'}, dimensions={0} | all-to-all | bytes 9830400 | tf_op jit(solution)/shard_map/all_to_all | solution.py:113
  140.1 5.9 %reshape.63 = bf16[480,5120]{1,0:T(8,128)(2,1)} reshape(bf16[32,15,5120]{2,1,0:T(8,128)(2,1)} %all_to_all.15) | data formatting | bytes 9830400 | tf_op jit(solution)/shard_map/reshape | solution.py:120
  146.0 6.2 %fusion.12 = f32[480,384]{1,0:T(8,128)S(1)} fusion(bf16[480,5120]{1,0:T(8,128)(2,1)} %reshape.63, bf16[1,5120,384]{2,1,0:T(8,128)(2,1)} %param.16), kind=kOutput, calls=%fused_computation.24 | convolution fusion | flops 1887436800 | bytes 9584640 | tf_op jit(solution)/shard_map/dot_general | solution.py:59
  152.3 0.4 copy-done.4
  152.7 3.6 %multiply_convert_fusion.4 = (bf16[480,384]{1,0:T(8,128)(2,1)S(1)}, f32[480,384]{1,0:T(8,128)}) fusion(f32[480,384]{1,0:T(8,128)S(1)} %fusion.12, bf16[480,5120]{1,0:T(8,128)(2,1)S(1)} %copy-done.1, bf16[1,5120,384]{2,1,0:T(8,128)(2,1)S(1)} %copy-done.4), kind=kOutput, calls=%fused_computation.40 | convolution fusion | flops 1888542720 | bytes 10690560 | tf_op jit(solution)/shard_map/dot_general | solution.py:60
  156.2 4.4 %convolution_convert_fusion.1 = bf16[480,5120]{1,0:T(8,128)(2,1)} fusion(bf16[480,384]{1,0:T(8,128)(2,1)S(1)} %get-tuple-element.49, bf16[1,384,5120]{2,1,0:T(8,128)(2,1)S(1)} %copy-done.5), kind=kOutput, calls=%fused_computation.3 | convolution fusion | flops 1889894400 | bytes 9216000 | tf_op jit(solution)/shard_map/dot_general | solution.py:64
  160.7 3.1 fusion.5
  163.8 3.0 multiply_convert_fusion.11
  166.8 0.6 copy-done.2
  167.5 3.5 convolution_convert_fusion.8
  171.0 3.0 pad_maximum_fusion.1
  174.0 0.2 reduce-scatter.7.cloned.1.call-start
  174.3 0.4 copy-done.3
  174.7 2.1 convolution_convert_fusion.2
  176.9 3.0 fusion.14
  179.9 1.2 convolution_convert_fusion.3
  181.1 1.2 convolution_convert_fusion.4
  182.4 13.7 %pad_maximum_fusion = bf16[5120,1152]{0,1:T(8,128)(2,1)} fusion(bf16[5120,384]{0,1:T(8,128)(2,1)S(1)} %convolution_convert_fusion.2, bf16[5120,384]{0,1:T(8,128)(2,1)S(1)} %convolution_convert_fusion.3, bf16[5120,384]{0,1:T(8,128)(2,1)S(1)} %convolution_convert_fusion.4), kind=kLoop, calls=%fused_computation | loop fusion | flops 35389440 | bytes 23592960 | tf_op jit(solution)/shard_map/concatenate | solution.py:134
  196.1 15.1 %copy.57 = bf16[5120,1152]{1,0:T(8,128)(2,1)} copy(bf16[5120,1152]{0,1:T(8,128)(2,1)} %pad_maximum_fusion) | data formatting | bytes 23592960
  211.4 3.6 %multiply_convert_fusion = bf16[480,5120]{1,0:T(8,128)(2,1)} fusion(pred[480,128]{1,0:T(8,128)(4,1)S(1)} %fusion.21, f32[480]{0:T(512)S(1)} %get-tuple-element.42, bf16[256,5120]{1,0:T(8,128)(2,1)S(1)} %copy-done), kind=kOutput, calls=%fused_computation.1 | convolution fusion | flops 634060800 | bytes 6289408 | tf_op jit(solution)/shard_map/dot_general | solution.py:110
  215.0 5.9 %reshape.66 = bf16[32,15,5120]{2,1,0:T(8,128)(2,1)} reshape(bf16[480,5120]{1,0:T(8,128)(2,1)} %multiply_convert_fusion) | data formatting | bytes 9830400 | tf_op jit(solution)/shard_map/reshape | solution.py:117
  220.9 70.2 %all_to_all.16 = bf16[32,15,5120]{2,1,0:T(8,128)(2,1)} all-to-all(bf16[32,15,5120]{2,1,0:T(8,128)(2,1)} %reshape.66), channel_id=1, replica_groups=mesh['tp'=4,'ep'=32] {'ep'}, dimensions={0} | all-to-all | bytes 9830400 | tf_op jit(solution)/shard_map/all_to_all | solution.py:116
  291.2 6.3 %reshape.67 = bf16[480,5120]{1,0:T(8,128)(2,1)} reshape(bf16[32,15,5120]{2,1,0:T(8,128)(2,1)} %all_to_all.16) | data formatting | bytes 9830400 | tf_op jit(solution)/shard_map/reshape | solution.py:121
  297.5 6.2 %fusion.7 = f32[480,384]{1,0:T(8,128)S(1)} fusion(bf16[480,5120]{1,0:T(8,128)(2,1)} %reshape.67, bf16[1,384,5120]{2,1,0:T(8,128)(2,1)} %param.18), kind=kOutput, calls=%fused_computation.19 | convolution fusion | flops 1887436800 | bytes 9584640 | tf_op jit(solution)/shard_map/dot_general | solution.py:67
  303.7 4.6 %fusion.1 = bf16[1,5120,384]{2,1,0:T(8,128)(2,1)} fusion(bf16[480,5120]{1,0:T(8,128)(2,1)S(1)} %bitcast.91, f32[480,384]{1,0:T(8,128)S(1)} %fusion.7, f32[480,384]{1,0:T(8,128)S(1)} %copy-done.10), kind=kOutput, calls=%fused_computation.11 | convolution fusion | flops 1890508800 | bytes 10321920 | tf_op jit(solution)/shard_map/dot_general | solution.py:33
  308.3 1.4 split.17
  309.7 1.3 convert_element_type.98
  311.0 4.1 %all-to-all-start.1 = ((bf16[32,15,1280]{2,1,0:T(8,128)(2,1)}), bf16[32,15,1280]{2,1,0:T(8,128)(2,1)S(1)}, u32[]{:S(2)}, u32[]{:S(2)}) async-start(bf16[32,15,1280]{2,1,0:T(8,128)(2,1)} %convert_element_type.98), calls=%async_computation.2 | async-start | bytes 2621440 | tf_op jit(solution)/shard_map/all_to_all | solution.py:157
  315.1 6.8 %fusion.2 = bf16[1,384,5120]{2,1,0:T(8,128)(2,1)} fusion(bf16[480,384]{1,0:T(8,128)(2,1)S(1)} %get-tuple-element.49, bf16[480,5120]{1,0:T(8,128)(2,1)} %reshape.67), kind=kOutput, calls=%fused_computation.12 | convolution fusion | flops 1889402880 | bytes 9216000 | tf_op jit(solution)/shard_map/dot_general | solution.py:33
  322.0 4.7 %fusion = bf16[1,5120,384]{2,1,0:T(8,128)(2,1)} fusion(bf16[480,5120]{1,0:T(8,128)(2,1)S(1)} %bitcast.93, f32[480,384]{1,0:T(8,128)S(1)} %copy-done.11, f32[480,384]{1,0:T(8,128)S(1)} %copy-done.8, f32[480,384]{1,0:T(8,128)S(1)} %copy-done.12), kind=kOutput, calls=%fused_computation.10 | convolution fusion | flops 1891246080 | bytes 11059200 | tf_op jit(solution)/shard_map/dot_general | solution.py:33
  326.7 7.8 %all-to-all-done.1 = bf16[32,15,1280]{2,1,0:T(8,128)(2,1)S(1)} async-done(((bf16[32,15,1280]{2,1,0:T(8,128)(2,1)}), bf16[32,15,1280]{2,1,0:T(8,128)(2,1)S(1)}, u32[]{:S(2)}, u32[]{:S(2)}) %all-to-all-start.1) | async-done | bytes 1228832 | tf_op jit(solution)/shard_map/all_to_all | solution.py:157
  334.4 0.4 reshape.64
  334.9 0.4 fusion.45
  335.2 0.4 convolution_add_fusion.1
  335.6 2.1 fusion.18
  337.7 9.1 %reduce-scatter.7.cloned.1.call-done = bf16[160,1152]{1,0:T(8,128)(2,1)} async-done(((bf16[5120,1152]{1,0:T(8,128)(2,1)}), bf16[160,1152]{1,0:T(8,128)(2,1)}) %reduce-scatter.7.cloned.1.call-update) | async-done | bytes 368656
  346.8 1.8 slice_bitcast_fusion
  (55 shorter events, 0.9 us)
Async XLA Ops:
  7.2 41.2 %all-gather.3.cloned.1.call-start = ((), (), s32[]{:S(2)}) async-start(), calls=%async_computation.5 | async-start | bytes 3276800 | tf_op jit(solution)/shard_map/all_gather | solution.py:10
  9.2 151.5 %all-gather.5.cloned.1.call-start = ((), (), s32[]{:S(2)}) async-start(), calls=%async_computation.6 | async-start | bytes 12165120 | tf_op jit(solution)/shard_map/all_gather | solution.py:17
  11.1 297.3 %reduce-scatter.5.cloned.1.call-start = ((), (), s32[]{:S(2)}) async-start(), calls=%async_computation.7 | async-start | bytes 7782400 | tf_op jit(solution)/shard_map/reduce_scatter | solution.py:28
  146.0 6.3 %copy-start.1 = (bf16[480,5120]{1,0:T(8,128)(2,1)S(1)}, bf16[480,5120]{1,0:T(8,128)(2,1)}, u32[]{:S(2)}) copy-start(bf16[480,5120]{1,0:T(8,128)(2,1)} %reshape.63) | copy-start | bytes 14745604
  146.0 6.7 %copy-start.4 = (bf16[1,5120,384]{2,1,0:T(8,128)(2,1)S(1)}, bf16[1,5120,384]{2,1,0:T(8,128)(2,1)}, u32[]{:S(2)}) copy-start(bf16[1,5120,384]{2,1,0:T(8,128)(2,1)} %param.17) | copy-start | bytes 11796484
  152.7 3.6 %copy-start.9 = (f32[480,384]{1,0:T(8,128)}, f32[480,384]{1,0:T(8,128)S(1)}, u32[]{:S(2)}) copy-start(f32[480,384]{1,0:T(8,128)S(1)} %fusion.12) | copy-start | bytes 2211844
  152.7 3.6 %copy-start.5 = (bf16[1,384,5120]{2,1,0:T(8,128)(2,1)S(1)}, bf16[1,384,5120]{2,1,0:T(8,128)(2,1)}, u32[]{:S(2)}) copy-start(bf16[1,384,5120]{2,1,0:T(8,128)(2,1)} %param.18) | copy-start | bytes 11796484
  156.2 4.4 %copy-start = (bf16[256,5120]{1,0:T(8,128)(2,1)S(1)}, bf16[256,5120]{1,0:T(8,128)(2,1)}, u32[]{:S(2)}) copy-start(bf16[256,5120]{1,0:T(8,128)(2,1)} %all-gather.3.cloned.1.call-done) | copy-start | bytes 7864324
  160.7 10.3 %slice-start.4 = ((s8[4915200]{0:T(1024)(128)(4,1)}), s8[4194304]{0:T(1024)(128)(4,1)S(1)}, s32[]{:S(2)}) async-start(s8[4915200]{0:T(1024)(128)(4,1)} %bitcast.94), calls=%async_computation.13 | async-start | bytes 8388608
  163.8 7.2 %slice-start.5 = ((s8[4915200]{0:T(1024)(128)(4,1)}), s8[720896]{0:T(1024)(128)(4,1)S(1)}, s32[]{:S(2)}) async-start(s8[4915200]{0:T(1024)(128)(4,1)} %bitcast.94), calls=%async_computation.14 | async-start | bytes 1441792
  166.8 0.6 copy-start.2
  174.0 0.7 copy-start.3
  174.0 0.7 copy-start.6
  174.0 172.7 %reduce-scatter.7.cloned.1.call-start = ((), (), s32[]{:S(2)}) async-start(), calls=%async_computation.8 | async-start | bytes 12165120
  291.1 12.5 %slice-start = ((s8[4915200]{0:T(1024)(128)(4,1)}), s8[720896]{0:T(1024)(128)(4,1)S(1)}, s32[]{:S(2)}) async-start(s8[4915200]{0:T(1024)(128)(4,1)} %bitcast.90), calls=%async_computation.9 | async-start | bytes 1441792
  297.5 6.2 %slice-start.1 = ((s8[4915200]{0:T(1024)(128)(4,1)}), s8[4194304]{0:T(1024)(128)(4,1)S(1)}, s32[]{:S(2)}) async-start(s8[4915200]{0:T(1024)(128)(4,1)} %bitcast.90), calls=%async_computation.10 | async-start | bytes 8388608
  297.5 6.2 %copy-start.10 = (f32[480,384]{1,0:T(8,128)S(1)}, f32[480,384]{1,0:T(8,128)}, u32[]{:S(2)}) copy-start(f32[480,384]{1,0:T(8,128)} %copy-done.9) | copy-start | bytes 2211844
  303.7 4.6 %copy-start.7 = (f32[480,384]{1,0:T(8,128)}, f32[480,384]{1,0:T(8,128)S(1)}, u32[]{:S(2)}) copy-start(f32[480,384]{1,0:T(8,128)S(1)} %fusion.7) | copy-start | bytes 2211844
  309.7 12.2 %slice-start.2 = ((s8[4915200]{0:T(1024)(128)(4,1)}), s8[720896]{0:T(1024)(128)(4,1)S(1)}, s32[]{:S(2)}) async-start(s8[4915200]{0:T(1024)(128)(4,1)} %bitcast.92), calls=%async_computation.11 | async-start | bytes 1441792
  311.0 23.4 %all-to-all-start.1 = ((bf16[32,15,1280]{2,1,0:T(8,128)(2,1)}), bf16[32,15,1280]{2,1,0:T(8,128)(2,1)S(1)}, u32[]{:S(2)}, u32[]{:S(2)}) async-start(bf16[32,15,1280]{2,1,0:T(8,128)(2,1)} %convert_element_type.98), calls=%async_computation.2 | async-start | bytes 2621440 | tf_op jit(solution)/shard_map/all_to_all | solution.py:157
  315.1 6.9 %slice-start.3 = ((s8[4915200]{0:T(1024)(128)(4,1)}), s8[4194304]{0:T(1024)(128)(4,1)S(1)}, s32[]{:S(2)}) async-start(s8[4915200]{0:T(1024)(128)(4,1)} %bitcast.92), calls=%async_computation.12 | async-start | bytes 8388608
  315.1 6.9 %copy-start.8 = (f32[480,384]{1,0:T(8,128)S(1)}, f32[480,384]{1,0:T(8,128)}, u32[]{:S(2)}) copy-start(f32[480,384]{1,0:T(8,128)} %copy-done.7) | copy-start | bytes 2211844
  315.1 6.9 %copy-start.11 = (f32[480,384]{1,0:T(8,128)S(1)}, f32[480,384]{1,0:T(8,128)}, u32[]{:S(2)}) copy-start(f32[480,384]{1,0:T(8,128)} %copy-done.9) | copy-start | bytes 2211844
  315.1 6.9 %copy-start.12 = (f32[480,384]{1,0:T(8,128)S(1)}, f32[480,384]{1,0:T(8,128)}, u32[]{:S(2)}) copy-start(f32[480,384]{1,0:T(8,128)} %get-tuple-element.50) | copy-start | bytes 2211844
Sparse Core Ops, SparseCore 0:
  10.2 38.1 all-gather.2
  51.2 105.1 all-gather.4
  174.2 62.7 reduce-scatter.4
  240.7 106.0 reduce-scatter.6
where the time goes:
time: 357 us; the launch traced here: 355 us
  blocking collectives  151 us (42%)
  matrix products  65.2 us (18%)
  waiting for transfers between devices  50.6 us (14%)
  local copies, waits for them, and re-layouts  47.2 us (13%)
  other arithmetic  22.5 us (6%)
  between operations  14 us (4%)
  starting transfers between devices  4.39 us (1%)
    all_to_all x1, blocking collectives, shards(): lax.all_to_all(rows_x.reshape(ep_count, -1, width), 'ep', split_axis=0, c...  80.9 us
    all_to_all x1, blocking collectives, shards(): lax.all_to_all(rows_dout.reshape(ep_count, -1, width), 'ep', split_axis=0...  70.2 us
    all_gather x1, waiting for transfers between devices, sent_together(): whole = lax.all_gather(both, axis, axis=dim, tiled=True)  33.7 us
    dot_general x6, matrix products, contract_rows(): lax.dot_general(left, right, (((0,), (0,)), ((), ())), preferred_element_...  20.8 us
    unnamed x40, local copies, waits for them, and re-layouts  17.5 us
    concatenate x1, other arithmetic, shards(): jnp.concatenate([contract_rows(x_full, shadow_gate_pre), contract_rows(x_...  13.7 us
    dot_general x2, matrix products, expert_pass(): pre_gate = jnp.dot(rows_x, weight_gate, preferred_element_type=jnp.float32)  9.35 us
    dot_general x2, matrix products, expert_pass(): lax.dot_general(rows_dout, weight_down, (((1,), (1,)), ((), ())), preferr...  9.18 us
  transfers between devices with their start and end apart: 5, of which 3 were waited for; matrix products, arithmetic and copies ran while one was open for 33% of the time, Pallas kernels for 0%

commit v1 on v0

v1 whole, which is shorter than its diff:
```python
import jax
import jax.numpy as jnp
from jax import lax
from jax.experimental import pallas as pl
from jax.experimental.pallas import tpu as pltpu
from jax.sharding import PartitionSpec as P

SLOTS = 16
MIX = 13
ROWS = 64
ANY = pl.BlockSpec(memory_space=pl.ANY)
VMEM = pl.BlockSpec(memory_space=pltpu.VMEM)
MESH = pl.DeviceIdType.MESH
BF16, F32 = jnp.bfloat16, jnp.float32


def contract_rows(left, right):
    return lax.dot_general(left, right, (((0,), (0,)), ((), ())), preferred_element_type=F32)


def split_parts(values):
    upper = values.astype(BF16)
    return upper, (values - upper.astype(F32)).astype(BF16)


def ep_peer(ep, k, sign):
    k = (k * MIX) % 32
    z, y, c = ep // 8, (ep // 2) % 4, ep % 2
    dz, dy, dc = k // 8, (k // 2) % 4, k % 2
    return ((z + sign * dz + 4) % 4) * 8 + ((y + sign * dy + 4) % 4) * 2 + (c + dc) % 2


def drain(ref, sem):
    pltpu.make_async_copy(ref, ref, sem).wait()


def dispatch_kernel(tok, cot, rows_x, rows_d, disp, gate, out_x, out_d, full_x, full_d, tok2, cot2, rows2_x, rows2_d,
                    ring_send, ring_recv, own_sem, a_send, a_recv, b_send, b_recv, f_send, f_recv):
    tp, ep = lax.axis_index("tp"), lax.axis_index("ep")
    quarter = tok.shape[1]
    mine = pl.multiple_of(tp * quarter, quarter)
    opposite = pl.multiple_of(((tp + 2) % 4) * quarter, quarter)
    my_rows = pl.multiple_of(ep * SLOTS, SLOTS)

    barrier = pltpu.get_barrier_semaphore()
    for d in (1, 2, 3):
        pl.semaphore_signal(barrier, inc=1, device_id=((tp + d) % 4, ep), device_id_type=MESH)

    def greet(k, carry):
        pl.semaphore_signal(barrier, inc=1, device_id=(tp, ep_peer(ep, k, 1)), device_id_type=MESH)
        return carry

    lax.fori_loop(1, 32, greet, 0)
    pl.semaphore_wait(barrier, 34)

    ring = []
    for d in (2, 1, 3):
        for i, (src, far, full) in enumerate(((tok, tok2, full_x), (cot, cot2, full_d))):
            copy = pltpu.make_async_remote_copy(
                src_ref=src, dst_ref=far if d == 2 else full.at[:, pl.ds(mine, quarter)],
                send_sem=ring_send.at[d - 1, i], recv_sem=ring_recv.at[d - 1, i],
                device_id=((tp + d) % 4, ep), device_id_type=MESH)
            copy.start()
            ring.append((d, copy))

    def send_rows(src_x, src_d, column, send_sem, recv_sem):
        def one(k, carry):
            peer = ep_peer(ep, k, 1)
            theirs = pl.multiple_of(peer * SLOTS, SLOTS)
            for src, out in ((src_x, out_x), (src_d, out_d)):
                pltpu.make_async_remote_copy(
                    src_ref=src.at[pl.ds(theirs, SLOTS), :],
                    dst_ref=out.at[pl.ds(my_rows, SLOTS), pl.ds(column, quarter)],
                    send_sem=send_sem, recv_sem=recv_sem, device_id=(tp, peer), device_id_type=MESH).start()
            return carry
        lax.fori_loop(1, 32, one, 0)

    send_rows(rows_x, rows_d, mine, a_send, a_recv.at[ep])

    local = [
        pltpu.make_async_copy(tok, full_x.at[:, pl.ds(mine, quarter)], own_sem.at[0]),
        pltpu.make_async_copy(cot, full_d.at[:, pl.ds(mine, quarter)], own_sem.at[1]),
        pltpu.make_async_copy(rows_x.at[pl.ds(my_rows, SLOTS), :],
                              out_x.at[pl.ds(my_rows, SLOTS), pl.ds(mine, quarter)], own_sem.at[2]),
        pltpu.make_async_copy(rows_d.at[pl.ds(my_rows, SLOTS), :],
                              out_d.at[pl.ds(my_rows, SLOTS), pl.ds(mine, quarter)], own_sem.at[3]),
    ]
    for copy in local:
        copy.start()

    for d, copy in ring[:2]:
        copy.wait_recv()

    def select(c, carry):
        at = pl.ds(pl.multiple_of(c * 128, 128), 128)
        rows2_x[at, :] = jnp.dot(disp[at, :], tok2[...], preferred_element_type=F32).astype(BF16)
        rows2_d[at, :] = (gate[at, :] * jnp.dot(disp[at, :], cot2[...], preferred_element_type=F32)).astype(BF16)
        return carry

    lax.fori_loop(0, rows2_x.shape[0] // 128, select, 0)
    send_rows(rows2_x, rows2_d, opposite, b_send, b_recv)
    late = [
        pltpu.make_async_copy(tok2, full_x.at[:, pl.ds(opposite, quarter)], own_sem.at[4]),
        pltpu.make_async_copy(cot2, full_d.at[:, pl.ds(opposite, quarter)], own_sem.at[5]),
        pltpu.make_async_copy(rows2_x.at[pl.ds(my_rows, SLOTS), :],
                              out_x.at[pl.ds(my_rows, SLOTS), pl.ds(opposite, quarter)], own_sem.at[6]),
        pltpu.make_async_copy(rows2_d.at[pl.ds(my_rows, SLOTS), :],
                              out_d.at[pl.ds(my_rows, SLOTS), pl.ds(opposite, quarter)], own_sem.at[7]),
    ]
    for copy in late:
        copy.start()
    for copy in local:
        copy.wait()

    def forward(source):
        at = pl.ds(pl.multiple_of(source * SLOTS, SLOTS), SLOTS), pl.ds(mine, quarter)
        for i, d in enumerate((1, 3)):
            for out in (out_x, out_d):
                pltpu.make_async_remote_copy(
                    src_ref=out.at[at], dst_ref=out.at[at], send_sem=f_send.at[i], recv_sem=f_recv.at[i],
                    device_id=((tp + d) % 4, ep), device_id_type=MESH).start()

    forward(ep)

    def relay(k, carry):
        source = ep_peer(ep, k, -1)
        drain(out_x.at[pl.ds(0, SLOTS), pl.ds(0, 2 * quarter)], a_recv.at[source])
        forward(source)
        return carry

    lax.fori_loop(1, 32, relay, 0)

    for copy in late:
        copy.wait()
    for d, copy in ring[:2]:
        copy.wait_send()
    for d, copy in ring[2:]:
        copy.wait()
    others = out_x.at[pl.ds(0, 31 * SLOTS), pl.ds(0, 2 * quarter)]
    everything = out_x.at[:, pl.ds(0, 2 * quarter)]
    drain(others, a_send)
    drain(others, b_send)
    drain(others, b_recv)
    for i in range(2):
        drain(everything, f_send.at[i])
        drain(everything, f_recv.at[i])


def dispatch_rows(tok, cot, rows_x, rows_d, disp, gate):
    count, quarter = tok.shape
    slots = rows_x.shape[0]
    width = 4 * quarter
    dma = pltpu.SemaphoreType.DMA
    return pl.pallas_call(
        dispatch_kernel,
        out_shape=(jax.ShapeDtypeStruct((slots, width), BF16),) * 2 + (jax.ShapeDtypeStruct((count, width), BF16),) * 2,
        in_specs=[VMEM] * 6,
        out_specs=(ANY,) * 4,
        scratch_shapes=[pltpu.VMEM((count, quarter), BF16)] * 2 + [pltpu.VMEM((slots, quarter), BF16)] * 2
        + [dma((3, 2)), dma((3, 2)), dma((8,)), dma, dma((32,)), dma, dma, dma((2,)), dma((2,))],
        compiler_params=pltpu.CompilerParams(collective_id=0, has_side_effects=True),
        name="dispatch_rows",
    )(tok, cot, rows_x, rows_d, disp, gate)


def combine_kernel(routed, shadow, back, shadow_sum, passing, relayed, far, near, total, pass_send, pass_recv, far_send,
                   far_recv, near_send, near_recv, back_send, back_recv, own_sem):
    tp, ep = lax.axis_index("tp"), lax.axis_index("ep")
    quarter = back.shape[1]
    blocks = routed.shape[0] // ROWS
    steps = blocks + shadow.shape[0] // ROWS
    per = ROWS // SLOTS

    barrier = pltpu.get_barrier_semaphore()
    for d in (1, 3):
        pl.semaphore_signal(barrier, inc=1, device_id=((tp + d) % 4, ep), device_id_type=MESH)

    def greet(k, carry):
        pl.semaphore_signal(barrier, inc=1, device_id=(tp, ep_peer(ep, k, 1)), device_id_type=MESH)
        return carry

    lax.fori_loop(1, 32, greet, 0)
    pl.semaphore_wait(barrier, 33)

    def block(i):
        return (i + ep // per) % blocks

    def piece(i, owner):
        columns = pl.ds(pl.multiple_of((owner % 4) * quarter, quarter), quarter)
        if i < blocks:
            return routed.at[pl.ds(pl.multiple_of(block(i) * ROWS, ROWS), ROWS), columns]
        return shadow.at[pl.ds((i - blocks) * ROWS, ROWS), columns]

    def way(i):
        return 1 if i % 2 == 0 else 3

    def send(src, dst, sems, i, d):
        return pltpu.make_async_remote_copy(
            src_ref=src, dst_ref=dst.at[i], send_sem=sems[0].at[i], recv_sem=sems[1].at[i],
            device_id=((tp + d) % 4, ep), device_id_type=MESH)

    passes = [send(piece(i, tp + 2), passing, (pass_send, pass_recv), i, way(i)) for i in range(steps)]
    nears = [send(piece(i, tp + 4 - way(i)), near, (near_send, near_recv), i, 4 - way(i)) for i in range(steps)]
    fars = [send(relayed.at[i], far, (far_send, far_recv), i, way(i)) for i in range(steps)]

    def finish(i):
        fars[i].wait_recv()
        nears[i].wait_recv()
        result = piece(i, tp)[...].astype(F32) + far[i].astype(F32) + near[i].astype(F32)
        if i >= blocks:
            shadow_sum[pl.ds((i - blocks) * ROWS, ROWS), :] = result
            return
        total[i] = result.astype(BF16)
        for j in range(per):
            peer = block(i) * per + j
            source = total.at[i, pl.ds(j * SLOTS, SLOTS), :]
            target = back.at[pl.ds(pl.multiple_of(ep * SLOTS, SLOTS), SLOTS), :]

            @pl.when(peer != ep)
            def _():
                pltpu.make_async_remote_copy(src_ref=source, dst_ref=target, send_sem=back_send, recv_sem=back_recv,
                                             device_id=(tp, peer), device_id_type=MESH).start()

            @pl.when(peer == ep)
            def _():
                pltpu.make_async_copy(source, target, own_sem).start()

    for i in range(steps):
        passes[i].start()
    for i in range(steps):
        nears[i].start()
        passes[i].wait_recv()
        relayed[i] = (piece(i, tp + way(i))[...].astype(F32) + passing[i].astype(F32)).astype(BF16)
        fars[i].start()
        if i >= 2:
            finish(i - 2)
    finish(steps - 2)
    finish(steps - 1)

    for i in range(steps):
        passes[i].wait_send()
        nears[i].wait_send()
        fars[i].wait_send()
    drain(back.at[pl.ds(0, SLOTS), :], own_sem)
    drain(back.at[pl.ds(0, 31 * SLOTS), :], back_send)
    drain(back.at[pl.ds(0, 31 * SLOTS), :], back_recv)


def combine_rows(routed, shadow):
    slots, width = routed.shape
    count, quarter = shadow.shape[0], width // 4
    steps = (slots + count) // ROWS
    dma = pltpu.SemaphoreType.DMA
    return pl.pallas_call(
        combine_kernel,
        out_shape=(jax.ShapeDtypeStruct((slots, quarter), BF16), jax.ShapeDtypeStruct((count, quarter), F32)),
        in_specs=[VMEM] * 2,
        out_specs=(VMEM,) * 2,
        scratch_shapes=[pltpu.VMEM((steps, ROWS, quarter), BF16)] * 4 + [pltpu.VMEM((slots // ROWS, ROWS, quarter), BF16)]
        + [dma((steps,))] * 6 + [dma] * 3,
        compiler_params=pltpu.CompilerParams(collective_id=1, has_side_effects=True),
        name="combine_rows",
    )(routed, shadow)


def outer_kernel(x, d, gate, up, hidden, out):
    part = gate.shape[1]
    out[:, :part] = contract_rows(x[...], gate[...]).astype(BF16)
    out[:, part:2 * part] = contract_rows(x[...], up[...]).astype(BF16)
    out[:, 2 * part:] = contract_rows(d[...], hidden[...]).astype(BF16)


def shadow_grads(x, d, gate, up, hidden):
    count, width = x.shape
    part, tile = gate.shape[1], 640
    wide = pl.BlockSpec((count, tile), lambda i: (0, i))
    whole = pl.BlockSpec((count, part), lambda i: (0, 0))
    return pl.pallas_call(
        outer_kernel, grid=(width // tile,),
        out_shape=jax.ShapeDtypeStruct((width, 3 * part), BF16),
        in_specs=[wide, wide, whole, whole, whole],
        out_specs=pl.BlockSpec((tile, 3 * part), lambda i: (i, 0)),
        cost_estimate=pl.CostEstimate(flops=6 * count * width * part, bytes_accessed=6 * width * part, transcendentals=0),
        name="shadow_grads",
    )(x, d, gate, up, hidden)


def expert_pass(rows_x, rows_dout, weight_gate, weight_up, weight_down):
    pre_gate = jnp.dot(rows_x, weight_gate, preferred_element_type=F32)
    pre_up = jnp.dot(rows_x, weight_up, preferred_element_type=F32)
    sigmoid_gate = jax.nn.sigmoid(pre_gate)
    activated = pre_gate * sigmoid_gate
    hidden = (activated * pre_up).astype(BF16)
    partial_out = jnp.dot(hidden, weight_down, preferred_element_type=F32).astype(BF16)
    hidden_grad = lax.dot_general(rows_dout, weight_down, (((1,), (1,)), ((), ())), preferred_element_type=F32)
    grad_pre_gate = (hidden_grad * pre_up * sigmoid_gate * (1.0 + pre_gate * (1.0 - sigmoid_gate))).astype(BF16)
    grad_pre_up = (hidden_grad * activated).astype(BF16)
    return partial_out, hidden, grad_pre_gate, grad_pre_up


def shards(tokens, cotangent, expert_ids, gate_weights, shadow_mask, w_gate, w_up, w_down, s_gate, s_up, s_down):
    tok_count, top_count = expert_ids.shape
    quarter = tokens.shape[1]
    width = 4 * quarter
    experts = 32
    slot_count = experts * SLOTS
    s_all = lax.all_gather(jnp.concatenate([s_gate, s_up, s_down.T], axis=1), "ep", axis=0, tiled=True)

    picks = expert_ids.reshape(-1)
    onehot = (picks[:, None] == jnp.arange(experts, dtype=jnp.int32)[None, :]).astype(jnp.int32)
    rank = jnp.sum((jnp.cumsum(onehot, axis=0) - onehot) * onehot, axis=1)
    slot_index = (picks * SLOTS + rank).reshape(tok_count, top_count)
    matches = jnp.arange(slot_count, dtype=jnp.int32)[:, None, None] == slot_index[None, :, :]
    dispatch = jnp.any(matches, axis=2).astype(BF16)
    weighting = jnp.sum(jnp.where(matches, gate_weights[None, :, :top_count], 0.0), axis=2)
    slot_gate = jnp.sum(weighting, axis=1, keepdims=True)
    shadow_weight = gate_weights[:, top_count] * shadow_mask.astype(F32)

    rows_x = jnp.dot(dispatch, tokens, preferred_element_type=F32).astype(BF16)
    rows_d = (slot_gate * jnp.dot(dispatch, cotangent, preferred_element_type=F32)).astype(BF16)
    expert_x, expert_d, full_x, full_dy = dispatch_rows(tokens, cotangent, rows_x, rows_d, dispatch, slot_gate)

    partial_out, hidden, grad_pre_gate, grad_pre_up = expert_pass(expert_x, expert_d, w_gate[0], w_up[0], w_down[0])
    grad_gate = contract_rows(expert_x, grad_pre_gate).astype(BF16)[None]
    grad_up = contract_rows(expert_x, grad_pre_up).astype(BF16)[None]
    grad_down = contract_rows(hidden, expert_d).astype(BF16)[None]

    part = s_gate.shape[1]
    shadow_d = (shadow_weight[:, None] * full_dy.astype(F32)).astype(BF16)
    full_gate, full_up, full_down = s_all[:, :part], s_all[:, part:2 * part], s_all[:, 2 * part:].T
    shadow_out, shadow_hidden, shadow_pre_gate, shadow_pre_up = expert_pass(full_x, shadow_d, full_gate, full_up, full_down)
    shadow_sums = lax.psum_scatter(
        shadow_grads(full_x, shadow_d, shadow_pre_gate, shadow_pre_up, shadow_hidden), "ep", scatter_dimension=0, tiled=True)
    grad_s_gate = shadow_sums[:, :part]
    grad_s_up = shadow_sums[:, part:2 * part]
    grad_s_down = shadow_sums[:, 2 * part:].T

    back, shadow_sum = combine_rows(partial_out, shadow_out)
    upper, lower = split_parts(weighting.T)
    combined = jnp.dot(upper, back, preferred_element_type=F32) + jnp.dot(lower, back, preferred_element_type=F32)
    mixed = (combined + shadow_weight[:, None] * shadow_sum).astype(BF16)
    return mixed, grad_gate, grad_up, grad_down, grad_s_gate, grad_s_up, grad_s_down


def solution(mesh):
    return jax.shard_map(
        shards, mesh=mesh,
        in_specs=(P("ep", "tp"), P("ep", "tp"), P("ep", None), P("ep", None), P("ep"), P("ep", None, "tp"),
                  P("ep", None, "tp"), P("ep", "tp", None), P("ep", "tp"), P("ep", "tp"), P("tp", "ep")),
        out_specs=(P("ep", "tp"), P("ep", None, "tp"), P("ep", None, "tp"), P("ep", "tp", None), P("ep", "tp"),
                   P("ep", "tp"), P("tp", "ep")),
        check_vma=False)
```

time: 357 us -> 261 us (0.73)
  Pallas kernels: 0 us -> 173 us
  blocking collectives: 151 us -> 0 us
  waiting for transfers between devices: 50.6 us -> 3.62 us
  local copies, waits for them, and re-layouts: 47.2 us -> 4.36 us
  other arithmetic: 22.5 us -> 7.61 us
  matrix products: 65.2 us -> 56.2 us
  starting transfers between devices: 4.39 us -> 0.08 us
    pallas_call x0 -> x3, Pallas kernels: none -> 173 us  [the longest x1 98.5 us: dispatch_rows(): pl.pallas_call(dispatch_kernel, out_shape=(jax.ShapeDtypeStruct((slots, w...]
    all_to_all x2 -> x0, blocking collectives: 151 us -> none  [the longest x1 80.9 us: shards(): lax.all_to_all(rows_x.reshape(ep_count, -1, width), 'ep', split_axis=0, c...]
    all_gather x2 -> x1, waiting for transfers between devices: 33.7 us -> 0.02 us  [shards(): lax.all_gather(jnp.concatenate([s_gate, s_up, s_down.T], axis=1), 'ep', a...]
    reshape x5 -> x0, local copies, waits for them, and re-layouts: 24.4 us -> none  [the longest x1 6.34 us: shards(): expert_dout = recv_dout.reshape(-1, width)]
    concatenate x4 -> x1, other arithmetic: 20.5 us -> 1.83 us  [shards(): jnp.concatenate([s_gate, s_up, s_down.T], axis=1)]
    unnamed x40 -> x23, local copies, waits for them, and re-layouts: 17.5 us -> 0.84 us
    unnamed x5 -> x2, waiting for transfers between devices: 9.12 us -> 0.03 us
    all_to_all x1 -> x0, waiting for transfers between devices: 7.76 us -> none  [shards(): lax.all_to_all(expert_sum.reshape(ep_count, -1, quarter_width).astype(jnp...]
  transfers between devices with their start and end apart: 5 -> 2, of which waited for: 3 -> 1; matrix products, arithmetic and copies ran while one was open for 33% -> 21% of each run, Pallas kernels for 0% -> 63%
where the time goes in v1:
time: 261 us; the launch traced here: 259 us
  Pallas kernels  173 us (66%)
  matrix products  56.2 us (22%)
  between operations  14.3 us (5%)
  other arithmetic  7.61 us (3%)
  local copies, waits for them, and re-layouts  4.36 us (2%)
  waiting for transfers between devices  3.62 us (1%)
    pallas_call x1, Pallas kernels, dispatch_rows(): pl.pallas_call(dispatch_kernel, out_shape=(jax.ShapeDtypeStruct((slots, w...  98.5 us
    pallas_call x1, Pallas kernels, combine_rows(): pl.pallas_call(combine_kernel, out_shape=(jax.ShapeDtypeStruct((slots, qu...  64.4 us
    dot_general x3, matrix products, contract_rows(): lax.dot_general(left, right, (((0,), (0,)), ((), ())), preferred_element_...  13.5 us
    pallas_call x1, Pallas kernels, shadow_grads(): pl.pallas_call(outer_kernel, grid=(width // tile,), out_shape=jax.ShapeDt...  9.91 us
    dot_general x2, matrix products, expert_pass(): jnp.dot(hidden, weight_down, preferred_element_type=F32).astype(BF16)  9.43 us
    dot_general x2, matrix products, expert_pass(): pre_gate = jnp.dot(rows_x, weight_gate, preferred_element_type=F32)  9.24 us
    dot_general x2, matrix products, expert_pass(): pre_up = jnp.dot(rows_x, weight_up, preferred_element_type=F32)  8.99 us
    dot_general x2, matrix products, expert_pass(): lax.dot_general(rows_dout, weight_down, (((1,), (1,)), ((), ())), preferr...  6.63 us
  transfers between devices with their start and end apart: 2, of which 1 were waited for; matrix products, arithmetic and copies ran while one was open for 21% of the time, Pallas kernels for 63%

profile of v1, /device:TPU:1, one launch (start us, length us, event | category | flops | bytes accessed | tf_op | source)
XLA Modules:
  0.0 259.0 jit_solution(2628757560787090377)
XLA Ops:
  7.2 0.0 copy-start.2
  7.2 0.0 all-gather.2.cloned.1.call-start
  7.2 1.8 pad_maximum_fusion
  9.1 0.0 all-gather.2.cloned.1.call-update
  9.1 0.0 reduce-scatter.2.cloned.1.call-start
  9.1 0.8 copy.34
  9.9 0.2 eq.43
  10.1 0.2 eq.39
  10.3 0.9 reduce-window.6
  11.2 0.2 slice_reduce_fusion
  11.5 0.1 fusion.30
  11.6 0.2 reduce_sum.30
  11.8 0.1 copy.37
  11.9 0.7 multiply_add_fusion
  12.6 0.1 fusion.21
  12.7 0.7 convert_element_type.75.disp
  13.3 0.9 select_reduce_fusion.1
  14.2 0.9 copy.38.gate
  15.1 2.5 convolution_convert_fusion.5.rows_x
  17.6 1.6 fusion.17.rows_d
  19.2 98.5 %dispatch_rows.1 = (bf16[512,5120]{1,0:T(8,128)(2,1)}, bf16[512,5120]{1,0:T(8,128)(2,1)}, bf16[128,5120]{1,0:T(8,128)(2,1)}, bf16[128,5120]{1,0:T(8,128)(2,1)}) custom-call(bf16[128,1280]{1,0:T(8,128)(2,1)} %tok.1, bf16[128,1280]{1,0:T(8,128)(2,1)} %cot.1, bf16[512,1280]{1,0:T(8,128)(2,1)} %convolution_convert_fusion.5.rows_x, ...), custom_call_target="tpu_custom_call" | custom-call | tf_op jit(solution)/shard_map/dispatch_rows/pallas_call | solution.py:154
  117.7 0.7 bitcast_multiply_fusion
  118.4 1.7 multiply_convert_fusion.d
  120.1 0.0 copy-start
  120.1 0.0 all-gather.2.cloned.1.call-done
  120.2 3.8 %fusion.3 = f32[128,384]{1,0:T(8,128)S(1)} fusion(bf16[128,5120]{1,0:T(8,128)(2,1)} %get-tuple-element.14.x, bf16[5120,1152]{1,0:T(8,128)(2,1)} %all-gather.2.cloned.1.call-done), kind=kOutput, calls=%fused_computation.8 | convolution fusion | flops 503316480 | bytes 5439488 | tf_op jit(solution)/shard_map/dot_general | solution.py:290
  124.0 0.0 copy-done.1
  124.0 3.0 %fusion.5 = f32[128,384]{1,0:T(8,128)S(1)} fusion(bf16[128,5120]{1,0:T(8,128)(2,1)S(1)} %copy-done.1, bf16[5120,1152]{1,0:T(8,128)(2,1)} %all-gather.2.cloned.1.call-done), kind=kOutput, calls=%fused_computation.10 | convolution fusion | flops 503316480 | bytes 5439488 | tf_op jit(solution)/shard_map/dot_general | solution.py:289
  127.0 3.8 %multiply_convert_fusion.6 = (bf16[128,384]{1,0:T(8,128)(2,1)}, bf16[128,384]{1,0:T(8,128)(2,1)}, bf16[128,384]{1,0:T(8,128)(2,1)}) fusion(f32[128,384]{1,0:T(8,128)S(1)} %fusion.5, f32[128,384]{1,0:T(8,128)S(1)} %fusion.3, bf16[128,5120]{1,0:T(8,128)(2,1)S(1)} %multiply_convert_fusion.d, bf16[5120,1152]{1,0:T(8,128)(2,1)} %all-gather.2.cloned.1.call-done), kind=kOutput, calls=%fused_computation.43 | convolution fusion | flops 504053760 | bytes 5931008 | tf_op jit(solution)/shard_map/dot_general | solution.py:295
  130.8 9.9 %shadow_grads.1 = bf16[5120,1152]{1,0:T(8,128)(2,1)} custom-call(bf16[128,5120]{1,0:T(8,128)(2,1)} %get-tuple-element.14.x, bf16[128,5120]{1,0:T(8,128)(2,1)} %copy-done, bf16[128,384]{1,0:T(8,128)(2,1)} %get-tuple-element.22.gate, bf16[128,384]{1,0:T(8,128)(2,1)} %get-tuple-element.21.up, bf16[128,384]{1,0:T(8,128)(2,1)} %get-tuple-element.23.hidden), custom_call_target="tpu_custom_call" | custom-call | flops 1509949440 | bytes 11796480 | tf_op jit(solution)/shard_map/shadow_grads/pallas_call | solution.py:278
  140.7 0.0 reduce-scatter.2.cloned.1.call-update
  140.7 0.0 copy-start.4
  140.7 0.0 slice-start
  140.7 6.2 %fusion.12 = f32[512,384]{1,0:T(8,128)S(1)} fusion(bf16[512,5120]{1,0:T(8,128)(2,1)} %get-tuple-element.13, bf16[1,5120,384]{2,1,0:T(8,128)(2,1)} %param.16), kind=kOutput, calls=%fused_computation.17 | convolution fusion | flops 2013265920 | bytes 9961472 | tf_op jit(solution)/shard_map/dot_general | solution.py:289
  147.0 0.0 copy-start.5
  147.0 0.0 slice-start.1
  147.0 5.2 %multiply_convert_fusion.3 = (bf16[512,384]{1,0:T(8,128)(2,1)S(1)}, f32[512,384]{1,0:T(8,128)S(1)}) fusion(f32[512,384]{1,0:T(8,128)S(1)} %fusion.12, bf16[512,5120]{1,0:T(8,128)(2,1)} %get-tuple-element.13, bf16[1,5120,384]{2,1,0:T(8,128)(2,1)S(1)} %copy-done.4), kind=kOutput, calls=%fused_computation.33 | convolution fusion | flops 2014445568 | bytes 11141120 | tf_op jit(solution)/shard_map/dot_general | solution.py:290
  152.2 4.6 %convolution_convert_fusion.routed = bf16[512,5120]{1,0:T(8,128)(2,1)} fusion(bf16[512,384]{1,0:T(8,128)(2,1)S(1)} %get-tuple-element.27, bf16[1,384,5120]{2,1,0:T(8,128)(2,1)S(1)} %copy-done.5), kind=kOutput, calls=%fused_computation | convolution fusion | flops 2015887360 | bytes 9568256 | tf_op jit(solution)/shard_map/dot_general | solution.py:294
  156.8 4.2 %fusion.2 = bf16[1,384,5120]{2,1,0:T(8,128)(2,1)} fusion(bf16[512,384]{1,0:T(8,128)(2,1)S(1)} %get-tuple-element.27, bf16[512,5120]{1,0:T(8,128)(2,1)S(1)} %bitcast.84), kind=kOutput, calls=%fused_computation.6 | convolution fusion | flops 2015232000 | bytes 9568256 | tf_op jit(solution)/shard_map/dot_general | solution.py:18
  161.0 2.9 %fusion.7 = f32[512,384]{1,0:T(8,128)S(1)} fusion(bf16[512,5120]{1,0:T(8,128)(2,1)S(1)} %bitcast.84, bf16[1,384,5120]{2,1,0:T(8,128)(2,1)S(1)} %copy-done.5), kind=kOutput, calls=%fused_computation.12 | convolution fusion | flops 2013265920 | bytes 9961472 | tf_op jit(solution)/shard_map/dot_general | solution.py:295
  163.9 4.6 %fusion.1 = bf16[1,5120,384]{2,1,0:T(8,128)(2,1)} fusion(bf16[512,5120]{1,0:T(8,128)(2,1)S(1)} %bitcast.90, f32[512,384]{1,0:T(8,128)S(1)} %fusion.7, f32[512,384]{1,0:T(8,128)S(1)} %fusion.12), kind=kOutput, calls=%fused_computation.5 | convolution fusion | flops 2016411648 | bytes 10747904 | tf_op jit(solution)/shard_map/dot_general | solution.py:18
  168.6 4.7 %fusion = bf16[1,5120,384]{2,1,0:T(8,128)(2,1)} fusion(bf16[512,5120]{1,0:T(8,128)(2,1)S(1)} %bitcast.90, f32[512,384]{1,0:T(8,128)S(1)} %fusion.12, f32[512,384]{1,0:T(8,128)S(1)} %fusion.7, f32[512,384]{1,0:T(8,128)S(1)} %get-tuple-element.28), kind=kOutput, calls=%fused_computation.4 | convolution fusion | flops 2017198080 | bytes 11534336 | tf_op jit(solution)/shard_map/dot_general | solution.py:18
  173.2 4.8 %convolution_convert_fusion.4.shadow = bf16[128,5120]{1,0:T(8,128)(2,1)} fusion(bf16[128,384]{1,0:T(8,128)(2,1)S(1)} %copy-done.3, bf16[5120,1152]{1,0:T(8,128)(2,1)} %all-gather.2.cloned.1.call-done), kind=kOutput, calls=%fused_computation.7 | convolution fusion | flops 503971840 | bytes 5341184 | tf_op jit(solution)/shard_map/dot_general | solution.py:294
  178.1 64.4 %combine_rows.1 = (bf16[512,1280]{1,0:T(8,128)(2,1)}, f32[128,1280]{1,0:T(8,128)}) custom-call(bf16[512,5120]{1,0:T(8,128)(2,1)} %convolution_convert_fusion.routed, bf16[128,5120]{1,0:T(8,128)(2,1)} %convolution_convert_fusion.4.shadow), custom_call_target="tpu_custom_call" | custom-call | tf_op jit(solution)/shard_map/combine_rows/pallas_call | solution.py:254
  242.5 1.7 fusion.35
  244.2 2.6 fusion.19
  246.8 3.6 %reduce-scatter.2.cloned.1.call-done = bf16[160,1152]{1,0:T(8,128)(2,1)} async-done(((bf16[5120,1152]{1,0:T(8,128)(2,1)}), bf16[160,1152]{1,0:T(8,128)(2,1)}) %reduce-scatter.2.cloned.1.call-update) | async-done | bytes 368656 | tf_op jit(solution)/shard_map/reduce_scatter | solution.py:332
  250.4 1.8 slice_bitcast_fusion
  (19 shorter events, 0.1 us)
Async XLA Ops:
  7.2 10.4 %copy-start.2 = (bf16[128,1280]{1,0:T(8,128)(2,1)S(1)}, bf16[128,1280]{1,0:T(8,128)(2,1)}, u32[]{:S(2)}) copy-start(bf16[128,1280]{1,0:T(8,128)(2,1)} %cot.1) | copy-start | bytes 983044
  7.2 113.0 %all-gather.2.cloned.1.call-start = ((), (), s32[]{:S(2)}) async-start(), calls=%async_computation.1 | async-start | bytes 12165120 | tf_op jit(solution)/shard_map/all_gather | solution.py:307
  9.1 241.3 %reduce-scatter.2.cloned.1.call-start = ((), (), s32[]{:S(2)}) async-start(), calls=%async_computation.2 | async-start | bytes 12165120 | tf_op jit(solution)/shard_map/reduce_scatter | solution.py:332
  12.6 105.1 %copy-start.6 = (s32[128]{0:T(128)S(1)}, s32[128]{0:T(128)}, u32[]{:S(2)}) copy-start(s32[128]{0:T(128)} %param.15) | copy-start | bytes 1540
  118.4 5.6 %copy-start.1 = (bf16[128,5120]{1,0:T(8,128)(2,1)S(1)}, bf16[128,5120]{1,0:T(8,128)(2,1)}, u32[]{:S(2)}) copy-start(bf16[128,5120]{1,0:T(8,128)(2,1)} %get-tuple-element.14.x) | copy-start | bytes 3932164
  120.1 6.9 %copy-start = (bf16[128,5120]{1,0:T(8,128)(2,1)}, bf16[128,5120]{1,0:T(8,128)(2,1)S(1)}, u32[]{:S(2)}) copy-start(bf16[128,5120]{1,0:T(8,128)(2,1)S(1)} %multiply_convert_fusion.d) | copy-start | bytes 3932164
  140.7 6.2 %copy-start.4 = (bf16[1,5120,384]{2,1,0:T(8,128)(2,1)S(1)}, bf16[1,5120,384]{2,1,0:T(8,128)(2,1)}, u32[]{:S(2)}) copy-start(bf16[1,5120,384]{2,1,0:T(8,128)(2,1)} %param.17) | copy-start | bytes 11796484
  140.7 16.0 %slice-start = ((s8[5242880]{0:T(1024)(128)(4,1)}), s8[4194304]{0:T(1024)(128)(4,1)S(1)}, s32[]{:S(2)}) async-start(s8[5242880]{0:T(1024)(128)(4,1)} %bitcast.83), calls=%async_computation.3 | async-start | bytes 8388608
  147.0 5.2 %copy-start.5 = (bf16[1,384,5120]{2,1,0:T(8,128)(2,1)S(1)}, bf16[1,384,5120]{2,1,0:T(8,128)(2,1)}, u32[]{:S(2)}) copy-start(bf16[1,384,5120]{2,1,0:T(8,128)(2,1)} %param.18) | copy-start | bytes 11796484
  147.0 9.8 %slice-start.1 = ((s8[5242880]{0:T(1024)(128)(4,1)}), s8[1048576]{0:T(1024)(128)(4,1)S(1)}, s32[]{:S(2)}) async-start(s8[5242880]{0:T(1024)(128)(4,1)} %bitcast.83), calls=%async_computation.4 | async-start | bytes 2097152
  156.8 7.1 %slice-start.2 = ((s8[5242880]{0:T(1024)(128)(4,1)}), s8[1048576]{0:T(1024)(128)(4,1)S(1)}, s32[]{:S(2)}) async-start(s8[5242880]{0:T(1024)(128)(4,1)} %bitcast.89), calls=%async_computation.5 | async-start | bytes 2097152
  161.0 2.9 %slice-start.3 = ((s8[5242880]{0:T(1024)(128)(4,1)}), s8[4194304]{0:T(1024)(128)(4,1)S(1)}, s32[]{:S(2)}) async-start(s8[5242880]{0:T(1024)(128)(4,1)} %bitcast.89), calls=%async_computation.6 | async-start | bytes 8388608
  168.6 4.7 %copy-start.3 = (bf16[128,384]{1,0:T(8,128)(2,1)S(1)}, bf16[128,384]{1,0:T(8,128)(2,1)}, u32[]{:S(2)}) copy-start(bf16[128,384]{1,0:T(8,128)(2,1)} %get-tuple-element.23.hidden) | copy-start | bytes 294916
Sparse Core Ops, SparseCore 0:
  10.8 107.9 all-gather.1
  140.8 109.4 reduce-scatter.1

commit v2 on v1

v2 whole, which is shorter than its diff:
```python
import jax
import jax.numpy as jnp
from jax import lax
from jax.experimental import pallas as pl
from jax.experimental.pallas import tpu as pltpu
from jax.sharding import PartitionSpec as P

SLOTS = 16
MIX = 13
ROWS = 64
CUTS = (0, 48, 80, 128, 160)
ORDER = sorted(((j, i) for j in range(4) for i in range(4) if j + i > 0), key=lambda ji: (ji[0] + ji[1], -ji[0]))
FIRST_LEG, E_START, W_PER = 6, 1, 1
VMEM_BYTES = 62 * 1024 * 1024
A_LEAD, A_RATE, R_START, R_RATE, R_MID = 4, 2, 5, 1, 20
ANY = pl.BlockSpec(memory_space=pl.ANY)
VMEM = pl.BlockSpec(memory_space=pltpu.VMEM)
MESH = pl.DeviceIdType.MESH
BF16, F32 = jnp.bfloat16, jnp.float32


def contract_rows(left, right):
    return lax.dot_general(left, right, (((0,), (0,)), ((), ())), preferred_element_type=F32)


def split_parts(values):
    upper = values.astype(BF16)
    return upper, (values - upper.astype(F32)).astype(BF16)


def ep_peer(ep, k, sign):
    k = (k * MIX) % 32
    z, y, c = ep // 8, (ep // 2) % 4, ep % 2
    dz, dy, dc = k // 8, (k // 2) % 4, k % 2
    return ((z + sign * dz + 4) % 4) * 8 + ((y + sign * dy + 4) % 4) * 2 + (c + dc) % 2


def drain(ref, sem):
    pltpu.make_async_copy(ref, ref, sem).wait()


def dispatch_kernel(tok, cot, disp, gate, s_gate, s_up, s_down, s_weight, out_x, out_d, out_s, out_g, full_x, full_d,
                    rows_x, rows_d, rows2_x, rows2_d, s_all, acc, hidden, slopes, stage, ring_send, ring_recv, own_sem,
                    a_send, a_recv, b_send, b_recv, f_send, f_recv, w_send, w_recv, pair_send, pair_recv, g_sem):
    tp, ep = lax.axis_index("tp"), lax.axis_index("ep")
    z, y, c = ep // 8, (ep // 2) % 4, ep % 2
    quarter, part, share = tok.shape[1], s_gate.shape[1], s_gate.shape[0]
    mine = pl.multiple_of(tp * quarter, quarter)
    opposite = pl.multiple_of(((tp + 2) % 4) * quarter, quarter)
    my_rows = pl.multiple_of(ep * SLOTS, SLOTS)
    partner = ep + 1 - 2 * c

    barrier = pltpu.get_barrier_semaphore()
    for d in (1, 2, 3):
        pl.semaphore_signal(barrier, inc=1, device_id=((tp + d) % 4, ep), device_id_type=MESH)

    def greet(k, carry):
        pl.semaphore_signal(barrier, inc=1, device_id=(tp, ep_peer(ep, k, 1)), device_id_type=MESH)
        return carry

    lax.fori_loop(1, 32, greet, 0)
    my_share = pl.ds(pl.multiple_of(ep * share, share), share)
    local = [pltpu.make_async_copy(src, s_all.at[my_share, pl.ds(i * part, part)], own_sem.at[i])
             for i, src in enumerate((s_gate, s_up, s_down))]
    local += [pltpu.make_async_copy(tok, full_x.at[:, pl.ds(mine, quarter)], own_sem.at[3]),
              pltpu.make_async_copy(cot, full_d.at[:, pl.ds(mine, quarter)], own_sem.at[4])]
    for copy in local:
        copy.start()
    pl.semaphore_wait(barrier, 34)

    ring = []
    for d in (2, 1, 3):
        for i, (src, full) in enumerate(((tok, full_x), (cot, full_d))):
            copy = pltpu.make_async_remote_copy(
                src_ref=src, dst_ref=full.at[:, pl.ds(mine, quarter)],
                send_sem=ring_send.at[d - 1, i], recv_sem=ring_recv.at[d - 1, i],
                device_id=((tp + d) % 4, ep), device_id_type=MESH)
            copy.start()
            ring.append(copy)

    def colour_step(q, at_first, at_second):
        sign = (1 - 2 * c) * (1 if q % 2 == 0 else -1)
        dz, dy = (at_second, at_first) if q < 2 else (at_first, at_second)
        return ((z + sign * dz + 8) % 4) * 8 + ((y + sign * dy + 8) % 4) * 2 + c

    def pass_on(q, j, i):
        origin = colour_step(q, -j, -i)
        where = s_all.at[pl.ds(pl.multiple_of(origin * share + CUTS[q], 16), CUTS[q + 1] - CUTS[q]), :]
        hops = []
        if i == 0 and j < 3:
            hops.append((colour_step(q, 1, 0), w_send.at[q], w_recv.at[q, (j + 1) * 4]))
        if i < 3:
            hops.append((colour_step(q, 0, 1), w_send.at[q], w_recv.at[q, j * 4 + i + 1]))
        hops.append((partner, pair_send, pair_recv))
        for peer, send_sem, recv_sem in hops:
            pltpu.make_async_remote_copy(src_ref=where, dst_ref=where, send_sem=send_sem, recv_sem=recv_sem,
                                         device_id=(tp, peer), device_id_type=MESH).start()

    for copy in local[:3]:
        copy.wait()
    for q in range(4):
        pass_on(q, 0, 0)

    def select(column, into_x, into_d):
        def one(r, carry):
            at = pl.ds(pl.multiple_of(r * 128, 128), 128)
            cut = pl.ds(column, quarter)
            into_x[at, :] = jnp.dot(disp[at, :], full_x[:, cut], preferred_element_type=F32).astype(BF16)
            into_d[at, :] = (gate[at, :] * jnp.dot(disp[at, :], full_d[:, cut], preferred_element_type=F32)).astype(BF16)
            return carry
        lax.fori_loop(0, into_x.shape[0] // 128, one, 0)

    def send_rows(first, last, src_x, src_d, column, send_sem, recv_sem):
        def one(k, carry):
            peer = ep_peer(ep, k, 1)
            theirs = pl.multiple_of(peer * SLOTS, SLOTS)
            for src, out in ((src_x, out_x), (src_d, out_d)):
                pltpu.make_async_remote_copy(
                    src_ref=src.at[pl.ds(theirs, SLOTS), :],
                    dst_ref=out.at[pl.ds(my_rows, SLOTS), pl.ds(column, quarter)],
                    send_sem=send_sem, recv_sem=recv_sem, device_id=(tp, peer), device_id_type=MESH).start()
            return carry
        lax.fori_loop(first, last, one, 0)

    def keep_rows(src_x, src_d, column, sems):
        copies = [pltpu.make_async_copy(src.at[pl.ds(my_rows, SLOTS), :],
                                        out.at[pl.ds(my_rows, SLOTS), pl.ds(column, quarter)], own_sem.at[sem])
                  for src, out, sem in ((src_x, out_x, sems), (src_d, out_d, sems + 1))]
        for copy in copies:
            copy.start()
        return copies

    def forward(source):
        at = pl.ds(pl.multiple_of(source * SLOTS, SLOTS), SLOTS), pl.ds(mine, quarter)
        for i, d in enumerate((1, 3)):
            for out in (out_x, out_d):
                pltpu.make_async_remote_copy(
                    src_ref=out.at[at], dst_ref=out.at[at], send_sem=f_send.at[i], recv_sem=f_recv.at[i],
                    device_id=((tp + d) % 4, ep), device_id_type=MESH).start()

    def relay(k, carry=0):
        source = ep_peer(ep, k, -1)
        drain(out_x.at[pl.ds(0, SLOTS), pl.ds(0, 2 * quarter)], a_recv.at[source])
        forward(source)
        return carry

    for copy in local[3:]:
        copy.wait()
    select(mine, rows_x, rows_d)
    kept = keep_rows(rows_x, rows_d, mine, 5)
    sent, relayed = 1, 1
    for r, (j, i) in enumerate(ORDER):
        upto = min(32, A_LEAD + A_RATE * (r + 1))
        if upto > sent:
            send_rows(sent, upto, rows_x, rows_d, mine, a_send, a_recv.at[ep])
            sent = upto
        for q in range(4):
            drain(s_all.at[pl.ds(0, CUTS[q + 1] - CUTS[q]), :], w_recv.at[q, j * 4 + i])
            pass_on(q, j, i)
        if r == 0:
            for copy in kept:
                copy.wait()
            forward(ep)
        if r >= R_START:
            lax.fori_loop(relayed, relayed + R_RATE, relay, 0)
            relayed += R_RATE

    for copy in ring[:2]:
        copy.wait_recv()
    select(opposite, rows2_x, rows2_d)
    send_rows(1, 32, rows2_x, rows2_d, opposite, b_send, b_recv)
    kept = keep_rows(rows2_x, rows2_d, opposite, 7)
    for copy in ring[2:]:
        copy.wait_recv()
    lax.fori_loop(relayed, R_MID, relay, 0)
    drain(s_all.at[pl.ds(0, s_all.shape[0] // 2), :], pair_recv)

    tile = 640
    tiles = full_x.shape[1] // tile
    left = (32 - R_MID) // tiles
    acc[...] = jnp.zeros_like(acc)

    def before(t, carry):
        at = pl.ds(pl.multiple_of(t * tile, tile), tile)
        full_d[:, at] = (s_weight[...] * full_d[:, at].astype(F32)).astype(BF16)
        acc[:, :2 * part] += jnp.dot(full_x[:, at], s_all[at, :2 * part], preferred_element_type=F32)
        acc[:, 2 * part:] += jnp.dot(full_d[:, at], s_all[at, 2 * part:], preferred_element_type=F32)
        lax.fori_loop(R_MID + t * left, R_MID + (t + 1) * left, relay, 0)
        return carry

    lax.fori_loop(0, tiles, before, 0)
    lax.fori_loop(R_MID + tiles * left, 32, relay, 0)
    pre_gate, pre_up, grad = acc[:, :part], acc[:, part:2 * part], acc[:, 2 * part:]
    sigmoid = jax.nn.sigmoid(pre_gate)
    active = pre_gate * sigmoid
    hidden[...] = (active * pre_up).astype(BF16)
    slopes[:, :part] = (grad * pre_up * sigmoid * (1.0 + pre_gate * (1.0 - sigmoid))).astype(BF16)
    slopes[:, part:] = (grad * active).astype(BF16)

    def after(t, carry):
        at = pl.ds(pl.multiple_of(t * tile, tile), tile)
        slot = t % 2
        result = pltpu.make_async_copy(stage.at[slot], out_g.at[at, :], g_sem.at[slot])

        @pl.when(t >= 2)
        def _():
            result.wait()

        out_s[:, at] = lax.dot_general(hidden[...], s_all[at, 2 * part:], (((1,), (1,)), ((), ())),
                                       preferred_element_type=F32).astype(BF16)
        stage[slot, :, :2 * part] = contract_rows(full_x[:, at], slopes[...]).astype(BF16)
        stage[slot, :, 2 * part:] = contract_rows(full_d[:, at], hidden[...]).astype(BF16)
        result.start()
        return carry

    lax.fori_loop(0, tiles, after, 0)
    for slot in range(2):
        drain(stage.at[slot], g_sem.at[slot])

    for copy in kept:
        copy.wait()
    for copy in ring:
        copy.wait_send()
    for q in range(4):
        drain(s_all.at[pl.ds(0, 15 * (CUTS[q + 1] - CUTS[q])), :], w_send.at[q])
    drain(s_all.at[pl.ds(0, s_all.shape[0] // 2), :], pair_send)
    others = out_x.at[pl.ds(0, 31 * SLOTS), pl.ds(0, 2 * quarter)]
    everything = out_x.at[:, pl.ds(0, 2 * quarter)]
    drain(others, a_send)
    drain(others, b_send)
    drain(others, b_recv)
    for i in range(2):
        drain(everything, f_send.at[i])
        drain(everything, f_recv.at[i])


def dispatch_rows(tok, cot, disp, gate, s_gate, s_up, s_down, s_weight):
    count, quarter = tok.shape
    slots, part = disp.shape[0], s_gate.shape[1]
    width = 4 * quarter
    dma = pltpu.SemaphoreType.DMA
    vmem = pltpu.VMEM
    return pl.pallas_call(
        dispatch_kernel,
        out_shape=(jax.ShapeDtypeStruct((slots, width), BF16),) * 2
        + (jax.ShapeDtypeStruct((count, width), BF16), jax.ShapeDtypeStruct((width, 3 * part), BF16)),
        in_specs=[VMEM] * 8,
        out_specs=(ANY, ANY, VMEM, ANY),
        scratch_shapes=[vmem((count, width), BF16)] * 2 + [vmem((slots, quarter), BF16)] * 4
        + [vmem((width, 3 * part), BF16), vmem((count, 3 * part), F32), vmem((count, part), BF16),
           vmem((count, 2 * part), BF16), vmem((2, 640, 3 * part), BF16)]
        + [dma((3, 2)), dma((3, 2)), dma((9,)), dma, dma((32,)), dma, dma, dma((2,)), dma((2,)), dma((4,)), dma((4, 16)),
           dma, dma, dma((2,))],
        compiler_params=pltpu.CompilerParams(collective_id=0, has_side_effects=True),
        name="dispatch_rows",
    )(tok, cot, disp, gate, s_gate, s_up, s_down, s_weight)


def combine_kernel(shadow, parts, rows_x, rows_d, w_gate, w_up, w_down, back, shadow_sum, share_out, grad_gate, grad_up,
                   grad_down, routed, all_x, all_d, down, strip_gate, strip_up, acc_gate, acc_up, acc_grad, hidden,
                   slope_gate, slope_up, passing, relayed, far, near, total, held, pair, arrived, put_gate, put_up,
                   put_down, pass_send, pass_recv, far_send, far_recv, near_send, near_recv, back_send,
                   back_recv, own_sem, pair_send, pair_recv, held_sem, s_send, s_recv, load_sem, put_sem):
    tp, ep = lax.axis_index("tp"), lax.axis_index("ep")
    z, y, c = ep // 8, (ep // 2) % 4, ep % 2
    quarter = back.shape[1]
    blocks = routed.shape[0] // ROWS
    steps = blocks + shadow.shape[0] // ROWS
    per = ROWS // SLOTS
    share = share_out.shape[0]
    tile = strip_gate.shape[1]
    tiles = rows_x.shape[1] // tile
    early = steps - blocks

    barrier = pltpu.get_barrier_semaphore()
    for d in (1, 3):
        pl.semaphore_signal(barrier, inc=1, device_id=((tp + d) % 4, ep), device_id_type=MESH)

    def greet(k, carry):
        pl.semaphore_signal(barrier, inc=1, device_id=(tp, ep_peer(ep, k, 1)), device_id_type=MESH)
        return carry

    lax.fori_loop(1, 32, greet, 0)

    def share_rows(chip, core):
        return parts.at[pl.ds(pl.multiple_of((chip * 2 + core) * share, share), share), :]

    def chip_at(k):
        return ((z + k // 4) % 4) * 4 + (y + k % 4) % 4

    def columns_of(t):
        return pl.ds(t * tile, tile)

    def loads(t):
        at, sem = columns_of(t), load_sem.at[t]
        return [pltpu.make_async_copy(src.at[:, at], dst.at[:, at], sem.at[i])
                for i, (src, dst) in enumerate(((rows_x, all_x), (rows_d, all_d), (w_down, down)))]

    def strips(t):
        return [pltpu.make_async_copy(src.at[columns_of(t), :], dst.at[t % 2], load_sem.at[t, 3 + i])
                for i, (src, dst) in enumerate(((w_gate, strip_gate), (w_up, strip_up)))]

    for t in range(tiles):
        for copy in loads(t) + (strips(t) if t < 2 else []):
            copy.start()

    def take(k, carry):
        chip = chip_at(k)
        pltpu.make_async_copy(share_rows(chip, c), held.at[chip], held_sem.at[chip]).start()
        return carry

    lax.fori_loop(0, 16, take, 0)
    pl.semaphore_wait(barrier, 33)

    def swap(k, carry):
        chip = chip_at(k)
        pltpu.make_async_remote_copy(
            src_ref=share_rows(chip, 1 - c), dst_ref=pair.at[chip], send_sem=pair_send, recv_sem=pair_recv.at[chip],
            device_id=(tp, ep + 1 - 2 * c), device_id_type=MESH).start()
        return carry

    lax.fori_loop(0, 16, swap, 0)

    def block(i):
        return (i + ep // per) % blocks

    def piece(i, owner):
        columns = pl.ds(pl.multiple_of((owner % 4) * quarter, quarter), quarter)
        if i >= early:
            return routed.at[pl.ds(pl.multiple_of(block(i) * ROWS, ROWS), ROWS), columns]
        return shadow.at[pl.ds(i * ROWS, ROWS), columns]

    def way(i):
        return 1 if i % 2 == 0 else 3

    def send(src, dst, sems, i, d):
        return pltpu.make_async_remote_copy(
            src_ref=src, dst_ref=dst.at[i], send_sem=sems[0].at[i], recv_sem=sems[1].at[i],
            device_id=((tp + d) % 4, ep), device_id_type=MESH)

    passes = [send(piece(i, tp + 2), passing, (pass_send, pass_recv), i, way(i)) for i in range(steps)]
    nears = [send(piece(i, tp + 4 - way(i)), near, (near_send, near_recv), i, 4 - way(i)) for i in range(steps)]
    fars = [send(relayed.at[i], far, (far_send, far_recv), i, way(i)) for i in range(steps)]

    def finish(i):
        fars[i].wait_recv()
        nears[i].wait_recv()
        result = piece(i, tp)[...].astype(F32) + far[i].astype(F32) + near[i].astype(F32)
        if i < early:
            shadow_sum[pl.ds(i * ROWS, ROWS), :] = result
            return
        total[i - early] = result.astype(BF16)
        for j in range(per):
            peer = block(i) * per + j
            source = total.at[i - early, pl.ds(j * SLOTS, SLOTS), :]
            target = back.at[pl.ds(pl.multiple_of(ep * SLOTS, SLOTS), SLOTS), :]

            @pl.when(peer != ep)
            def _():
                pltpu.make_async_remote_copy(src_ref=source, dst_ref=target, send_sem=back_send, recv_sem=back_recv,
                                             device_id=(tp, peer), device_id_type=MESH).start()

            @pl.when(peer == ep)
            def _():
                pltpu.make_async_copy(source, target, own_sem).start()

    def relay(i):
        passes[i].wait_recv()
        relayed[i] = (piece(i, tp + way(i))[...].astype(F32) + passing[i].astype(F32)).astype(BF16)
        fars[i].start()

    def ahead(t):
        for copy in loads(t) + strips(t):
            copy.wait()
        acc_gate[...] += jnp.dot(all_x[:, columns_of(t)], strip_gate[t % 2], preferred_element_type=F32)
        acc_up[...] += jnp.dot(all_x[:, columns_of(t)], strip_up[t % 2], preferred_element_type=F32)
        acc_grad[...] += lax.dot_general(all_d[:, columns_of(t)], down[:, columns_of(t)], (((1,), (1,)), ((), ())),
                                         preferred_element_type=F32)
        if t + 2 < tiles:
            for copy in strips(t + 2):
                copy.start()

    def activate():
        pre_gate, pre_up, grad = acc_gate[...], acc_up[...], acc_grad[...]
        sigmoid = jax.nn.sigmoid(pre_gate)
        active = pre_gate * sigmoid
        hidden[...] = (active * pre_up).astype(BF16)
        slope_gate[...] = (grad * pre_up * sigmoid * (1.0 + pre_gate * (1.0 - sigmoid))).astype(BF16)
        slope_up[...] = (grad * active).astype(BF16)

    def project(owner):
        at = pl.ds(pl.multiple_of((owner % 4) * quarter, quarter), quarter)
        routed[:, at] = jnp.dot(hidden[...], down[:, at], preferred_element_type=F32).astype(BF16)

    def puts(t):
        slot = t % 2
        return [pltpu.make_async_copy(put_gate.at[slot], grad_gate.at[columns_of(t), :], put_sem.at[slot, 0]),
                pltpu.make_async_copy(put_up.at[slot], grad_up.at[columns_of(t), :], put_sem.at[slot, 1]),
                pltpu.make_async_copy(put_down.at[slot], grad_down.at[:, columns_of(t)], put_sem.at[slot, 2])]

    def weights(t):
        slot = t % 2
        if t >= 2:
            for copy in puts(t - 2):
                copy.wait()
        put_gate[slot] = contract_rows(all_x[:, columns_of(t)], slope_gate[...]).astype(BF16)
        put_up[slot] = contract_rows(all_x[:, columns_of(t)], slope_up[...]).astype(BF16)
        put_down[slot] = contract_rows(hidden[...], all_d[:, columns_of(t)]).astype(BF16)
        for copy in puts(t):
            copy.start()

    def colour_step(q, at_first, at_second):
        sign = (1 - 2 * c) * (1 if q % 2 == 0 else -1)
        dz, dy = (at_second, at_first) if q < 2 else (at_first, at_second)
        return ((z + sign * dz + 8) % 4) * 4 + (y + sign * dy + 8) % 4

    def mine(q, a, b):
        return held.at[colour_step(q, -a, -b), pl.ds(CUTS[q], CUTS[q + 1] - CUTS[q]), :]

    def hand_on(q, a, b, along_first, event):
        peer = colour_step(q, 1, 0) if along_first else colour_step(q, 0, 1)
        pltpu.make_async_remote_copy(
            src_ref=mine(q, a, b), dst_ref=arrived.at[event, pl.ds(CUTS[q], CUTS[q + 1] - CUTS[q]), :],
            send_sem=s_send.at[q], recv_sem=s_recv.at[q, event], device_id=(tp, peer * 2 + c),
            device_id_type=MESH).start()

    def gather(q, a, b, event):
        rows = pl.ds(CUTS[q], CUTS[q + 1] - CUTS[q])
        drain(arrived.at[event, rows, :], s_recv.at[q, event])
        kept = mine(q, a, b)
        kept[...] = (kept[...].astype(F32) + arrived[event, rows, :].astype(F32)).astype(BF16)

    def first_leg(t, b):
        for q in range(4):
            gather(q, (t + 1) % 4, b, (t - 1) * 4 + b)
            if t < 3:
                hand_on(q, t + 1, b, True, t * 4 + b)
            elif b == 1:
                hand_on(q, 0, 1, False, 12)

    def second_leg(t):
        for q in range(4):
            gather(q, 0, (t + 1) % 4, 11 + t)
            if t < 3:
                hand_on(q, 0, t + 1, False, 12 + t)

    def join(k, carry):
        chip = chip_at(k)
        drain(held.at[chip], held_sem.at[chip])
        drain(pair.at[chip], pair_recv.at[chip])
        held[chip] = (held[chip].astype(F32) + pair[chip].astype(F32)).astype(BF16)
        return carry

    for i in range(early):
        passes[i].start()
    for i in range(early):
        nears[i].start()
    for ref in (acc_gate, acc_up, acc_grad):
        ref[...] = jnp.zeros_like(ref)
    plan = [lambda t=t, b=b: first_leg(t, b) for t in (1, 2, 3) for b in (1, 2, 3, 0)]
    plan = plan[:10] + [lambda: second_leg(1), plan[10], lambda: second_leg(2), plan[11], lambda: second_leg(3)]
    for t in range(tiles):
        if 1 <= t <= 4:
            lax.fori_loop(4 * t - 4, 4 * t, join, 0)
        if t == 5:
            for b in (1, 2, 3, 0):
                for q in range(4):
                    hand_on(q, 1, b, True, b)
            for i in range(early):
                relay(i)
        ahead(t)
        if t >= FIRST_LEG and plan:
            plan.pop(0)()
    activate()
    project(tp + 2)
    for i in range(early, steps):
        passes[i].start()
    project(tp + 1)
    project(tp + 3)
    for i in range(early, steps):
        nears[i].start()
    project(tp)
    for i in range(early):
        finish(i)
    todo = [lambda i=i: relay(i) for i in range(early, steps)]
    ends = [lambda i=i: finish(i) for i in range(early, steps)]
    work = [lambda t=t: weights(t) for t in range(tiles)]
    while plan or todo or ends or work:
        for queue, count in ((work, W_PER), (plan, 1), (todo, 1)):
            for one in queue[:count]:
                one()
            del queue[:count]
        if len(plan) < E_START and len(todo) < len(ends):
            ends.pop(0)()
    final = pltpu.make_async_copy(held.at[z * 4 + y], share_out, own_sem)

    for i in range(steps):
        passes[i].wait_send()
        nears[i].wait_send()
        fars[i].wait_send()
    drain(back.at[pl.ds(0, SLOTS), :], own_sem)
    final.start()
    final.wait()
    for copy in puts(tiles - 2) + puts(tiles - 1):
        copy.wait()
    drain(held, pair_send)
    for q in range(4):
        drain(parts.at[pl.ds(0, 15 * (CUTS[q + 1] - CUTS[q])), :], s_send.at[q])
    drain(back.at[pl.ds(0, 31 * SLOTS), :], back_send)
    drain(back.at[pl.ds(0, 31 * SLOTS), :], back_recv)


def combine_rows(shadow, parts, rows_x, rows_d, w_gate, w_up, w_down):
    (slots, width), (count, _) = rows_x.shape, shadow.shape
    quarter, part, share, steps, tile = width // 4, w_gate.shape[1], width // 32, (slots + count) // ROWS, 512
    dma, vmem, like = pltpu.SemaphoreType.DMA, pltpu.VMEM, jax.ShapeDtypeStruct
    return pl.pallas_call(
        combine_kernel,
        out_shape=(like((slots, quarter), BF16), like((count, quarter), F32), like((share, 3 * part), BF16),
                   like((width, part), BF16), like((width, part), BF16), like((part, width), BF16)),
        in_specs=[VMEM] + [ANY] * 6,
        out_specs=(VMEM, VMEM, VMEM, ANY, ANY, ANY),
        scratch_shapes=[vmem((slots, width), BF16)] * 3 + [vmem((part, width), BF16)] + [vmem((2, tile, part), BF16)] * 2
        + [vmem((slots, part), F32)] * 3 + [vmem((slots, part), BF16)] * 3
        + [vmem((steps, ROWS, quarter), BF16)] * 4 + [vmem((slots // ROWS, ROWS, quarter), BF16)]
        + [vmem((16, share, 3 * part), BF16)] * 2 + [vmem((15, share, 3 * part), BF16)]
        + [vmem((2, tile, part), BF16)] * 2 + [vmem((2, part, tile), BF16)]
        + [dma((steps,))] * 6 + [dma] * 3
        + [dma, dma((16,)), dma((16,)), dma((4,)), dma((4, 15)), dma((width // tile, 5)), dma((2, 3))],
        compiler_params=pltpu.CompilerParams(collective_id=1, has_side_effects=True, vmem_limit_bytes=VMEM_BYTES),
        name="combine_rows",
    )(shadow, parts, rows_x, rows_d, w_gate, w_up, w_down)


def shards(tokens, cotangent, expert_ids, gate_weights, shadow_mask, w_gate, w_up, w_down, s_gate, s_up, s_down):
    tok_count, top_count = expert_ids.shape
    quarter = tokens.shape[1]
    width = 4 * quarter
    experts = 32
    slot_count = experts * SLOTS
    picks = expert_ids.reshape(-1)
    onehot = (picks[:, None] == jnp.arange(experts, dtype=jnp.int32)[None, :]).astype(jnp.int32)
    rank = jnp.sum((jnp.cumsum(onehot, axis=0) - onehot) * onehot, axis=1)
    slot_index = (picks * SLOTS + rank).reshape(tok_count, top_count)
    matches = jnp.arange(slot_count, dtype=jnp.int32)[:, None, None] == slot_index[None, :, :]
    dispatch = jnp.any(matches, axis=2).astype(BF16)
    weighting = jnp.sum(jnp.where(matches, gate_weights[None, :, :top_count], 0.0), axis=2)
    slot_gate = jnp.sum(weighting, axis=1, keepdims=True)
    shadow_weight = gate_weights[:, top_count] * shadow_mask.astype(F32)

    expert_x, expert_d, shadow_out, shadow_part = dispatch_rows(
        tokens, cotangent, dispatch, slot_gate, s_gate, s_up, s_down.T, shadow_weight[:, None])
    part = s_gate.shape[1]

    back, shadow_sum, shadow_sums, grad_gate, grad_up, grad_down = combine_rows(
        shadow_out, shadow_part, expert_x, expert_d, w_gate[0], w_up[0], w_down[0])
    grad_gate, grad_up, grad_down = grad_gate[None], grad_up[None], grad_down[None]
    grad_s_gate = shadow_sums[:, :part]
    grad_s_up = shadow_sums[:, part:2 * part]
    grad_s_down = shadow_sums[:, 2 * part:].T

    upper, lower = split_parts(weighting.T)
    combined = jnp.dot(upper, back, preferred_element_type=F32) + jnp.dot(lower, back, preferred_element_type=F32)
    mixed = (combined + shadow_weight[:, None] * shadow_sum).astype(BF16)
    return mixed, grad_gate, grad_up, grad_down, grad_s_gate, grad_s_up, grad_s_down


def solution(mesh):
    return jax.shard_map(
        shards, mesh=mesh,
        in_specs=(P("ep", "tp"), P("ep", "tp"), P("ep", None), P("ep", None), P("ep"), P("ep", None, "tp"),
                  P("ep", None, "tp"), P("ep", "tp", None), P("ep", "tp"), P("ep", "tp"), P("tp", "ep")),
        out_specs=(P("ep", "tp"), P("ep", None, "tp"), P("ep", None, "tp"), P("ep", "tp", None), P("ep", "tp"),
                   P("ep", "tp"), P("tp", "ep")),
        check_vma=False)
```

time: 261 us -> 221 us (0.85)
  matrix products: 56.2 us -> 4.26 us
  Pallas kernels: 173 us -> 197 us
  between operations: 14.3 us -> 0.69 us
  local copies, waits for them, and re-layouts: 4.36 us -> 14.2 us
  waiting for transfers between devices: 3.62 us -> 0 us
  other arithmetic: 7.61 us -> 4.08 us
    dot_general x13 -> x0, matrix products: 51.9 us -> none  [the longest x3 13.5 us: contract_rows(): lax.dot_general(left, right, (((0,), (0,)), ((), ())), preferred_element_...]
    pallas_call x1, Pallas kernels: 98.5 us -> 112 us  [dispatch_rows(): pl.pallas_call(dispatch_kernel, out_shape=(jax.ShapeDtypeStruct((slots, w...]
    pallas_call x2 -> x1, Pallas kernels: 74.3 us -> 85.4 us  [combine_rows(): pl.pallas_call(combine_kernel, out_shape=(like((slots, quarter), BF16), l...]
    unnamed x23 -> x10, local copies, waits for them, and re-layouts: 0.84 us -> 9.78 us
    reduce_scatter x1 -> x0, waiting for transfers between devices: 3.57 us -> none  [shards(): lax.psum_scatter(shadow_grads(full_x, shadow_d, shadow_pre_gate, shadow_p...]
  transfers between devices with their start and end apart: 2 -> 0, of which waited for: 1 -> 0; matrix products, arithmetic and copies ran while one was open for 21% -> 0% of each run, Pallas kernels for 63% -> 0%
where the time goes in v2:
time: 221 us; the launch traced here: 220 us
  Pallas kernels  197 us (89%)
  local copies, waits for them, and re-layouts  14.2 us (6%)
  matrix products  4.26 us (2%)
  other arithmetic  4.08 us (2%)
    pallas_call x1, Pallas kernels, dispatch_rows(): pl.pallas_call(dispatch_kernel, out_shape=(jax.ShapeDtypeStruct((slots, w...  112 us
    pallas_call x1, Pallas kernels, combine_rows(): pl.pallas_call(combine_kernel, out_shape=(like((slots, quarter), BF16), l...  85.4 us
    unnamed x10, local copies, waits for them, and re-layouts  9.78 us

profile of v2, /device:TPU:1, one launch (start us, length us, event | category | flops | bytes accessed | tf_op | source)
XLA Modules:
  0.0 220.4 jit_solution(721173447061698214)
XLA Ops:
  0.6 0.7 bitcast_multiply_fusion
  1.3 0.8 copy.37
  2.1 0.2 eq.43
  2.3 0.2 eq.39
  2.6 0.9 reduce-window.6
  3.4 0.2 slice_reduce_fusion
  3.7 0.1 fusion.8
  3.8 0.2 reduce_sum.30
  4.0 0.1 copy.40
  4.1 0.7 multiply_add_fusion
  4.8 0.1 fusion.2
  4.9 0.7 convert_element_type.28.disp
  5.6 0.7 copy.42.s_weight
  6.3 0.9 select_reduce_fusion.1
  7.2 0.9 copy.41.gate
  8.0 111.8 %dispatch_rows.1 = (bf16[512,5120]{1,0:T(8,128)(2,1)}, bf16[512,5120]{1,0:T(8,128)(2,1)}, bf16[128,5120]{1,0:T(8,128)(2,1)}, bf16[5120,1152]{1,0:T(8,128)(2,1)}) custom-call(bf16[128,1280]{1,0:T(8,128)(2,1)} %tok.1, bf16[128,1280]{1,0:T(8,128)(2,1)} %cot.1, bf16[512,128]{1,0:T(8,128)(2,1)} %convert_element_type.28.disp, f32[512,1]{1,0:T(8,128)} %copy.41.gate, ...), custom_call_target="tpu_custom_call" | custom-call | tf_op jit(solution)/shard_map/dispatch_rows/pallas_call | solution.py:243
  119.8 85.4 %combine_rows.1 = (bf16[512,1280]{1,0:T(8,128)(2,1)}, f32[128,1280]{1,0:T(8,128)}, bf16[160,1152]{1,0:T(8,128)(2,1)}, bf16[5120,384]{1,0:T(8,128)(2,1)}, bf16[51...) custom-call(bf16[128,5120]{1,0:T(8,128)(2,1)} %get-tuple-element.17.shadow, bf16[5120,1152]{1,0:T(8,128)(2,1)} %get-tuple-element.18.parts, ...), custom_call_target="tpu_custom_call" | custom-call | tf_op jit(solution)/shard_map/combine_rows/pallas_call | solution.py:517
  205.2 0.0 copy-start.2
  205.3 1.9 slice_bitcast_fusion
  207.2 1.7 fusion.11
  208.9 2.6 %fusion.1 = bf16[128,1280]{1,0:T(8,128)(2,1)} fusion(f32[128,1280]{1,0:T(8,128)S(1)} %fusion.11, bf16[512,1280]{1,0:T(8,128)(2,1)} %get-tuple-element.21, f32[128,1280]{1,0:T(8,128)} %get-tuple-element.22, f32[128]{0:T(128)S(1)} %bitcast_multiply_fusion, f32[512,128]{1,0:T(8,128)S(1)} %get-tuple-element.27), kind=kOutput, calls=%fused_computation.2 | convolution fusion | flops 168689664 | bytes 3211776 | tf_op jit(solution)/shard_map/dot_general | solution.py:563
  211.4 0.0 copy-done.2
  211.4 0.0 copy-start.1
  211.4 2.0 copy.48
  213.4 1.5 copy-done.1
  215.0 0.0 copy-start
  215.0 2.0 copy.49
  217.0 1.5 copy-done
  218.5 1.9 copy.50
  (2 shorter events, 0.0 us)
Async XLA Ops:
  205.2 6.2 %copy-start.2 = (bf16[5120,384]{1,0:T(8,128)(2,1)S(1)}, bf16[5120,384]{1,0:T(8,128)(2,1)}, u32[]{:S(2)}) copy-start(bf16[5120,384]{1,0:T(8,128)(2,1)} %get-tuple-element.23) | copy-start | bytes 11796484
  211.4 3.5 %copy-start.1 = (bf16[5120,384]{1,0:T(8,128)(2,1)S(1)}, bf16[5120,384]{1,0:T(8,128)(2,1)}, u32[]{:S(2)}) copy-start(bf16[5120,384]{1,0:T(8,128)(2,1)} %get-tuple-element.24) | copy-start | bytes 11796484
  215.0 3.5 %copy-start = (bf16[384,5120]{1,0:T(8,128)(2,1)S(1)}, bf16[384,5120]{1,0:T(8,128)(2,1)}, u32[]{:S(2)}) copy-start(bf16[384,5120]{1,0:T(8,128)(2,1)} %get-tuple-element.25) | copy-start | bytes 11796484

commit v3 on v2

--- a/solution.py
+++ b/solution.py
@@ -10,9 +10,10 @@
 ROWS = 64
 CUTS = (0, 48, 80, 128, 160)
 ORDER = sorted(((j, i) for j in range(4) for i in range(4) if j + i > 0), key=lambda ji: (ji[0] + ji[1], -ji[0]))
-FIRST_LEG, E_START, W_PER = 6, 1, 1
+FIRST_LEG, E_START, W_PER = 10, 4, 1
 VMEM_BYTES = 62 * 1024 * 1024
-A_LEAD, A_RATE, R_START, R_RATE, R_MID = 4, 2, 5, 1, 20
+A_LEAD, A_RATE, R_START, R_RATE, R_MID = 16, 4, 2, 2, 28
+B_AT = 14
 ANY = pl.BlockSpec(memory_space=pl.ANY)
 VMEM = pl.BlockSpec(memory_space=pltpu.VMEM)
 MESH = pl.DeviceIdType.MESH
@@ -39,8 +40,41 @@
     pltpu.make_async_copy(ref, ref, sem).wait()
 
 
-def dispatch_kernel(tok, cot, disp, gate, s_gate, s_up, s_down, s_weight, out_x, out_d, out_s, out_g, full_x, full_d,
-                    rows_x, rows_d, rows2_x, rows2_d, s_all, acc, hidden, slopes, stage, ring_send, ring_recv, own_sem,
+def route(ids, gates, mask, disp, gate, s_weight, upper, lower):
+    count, slots = disp.shape[1], disp.shape[0]
+    experts = slots // SLOTS
+    expert = lax.broadcasted_iota(jnp.int32, (experts, count), 0)
+    picked = jnp.zeros((experts, count), F32)
+    given = jnp.zeros((experts, count), F32)
+    for j in range(ids.shape[0]):
+        hit = expert == ids[j:j + 1, :]
+        picked = picked + jnp.where(hit, 1.0, 0.0)
+        given = given + jnp.where(hit, gates[j:j + 1, :], 0.0)
+    first = lax.broadcasted_iota(jnp.int32, (count, count), 0)
+    second = lax.broadcasted_iota(jnp.int32, (count, count), 1)
+    earlier = jnp.where(first < second, 1.0, 0.0).astype(BF16)
+    rank = jnp.dot(picked.astype(BF16), earlier, preferred_element_type=F32)
+    slot = lax.broadcasted_iota(jnp.int32, (slots, experts), 0)
+    owner = lax.broadcasted_iota(jnp.int32, (slots, experts), 1)
+    spread = jnp.where(slot // SLOTS == owner, 1.0, 0.0).astype(BF16)
+
+    def widen(values):
+        return jnp.dot(spread, values.astype(BF16), preferred_element_type=F32)
+
+    place = (lax.broadcasted_iota(jnp.int32, (slots, count), 0) % SLOTS).astype(F32)
+    filled = jnp.where((widen(picked) > 0.5) & (widen(rank) == place), 1.0, 0.0)
+    top, rest = split_parts(given)
+    middle, last = split_parts(given - top.astype(F32) - rest.astype(F32))
+    weight = filled * ((widen(top) + widen(rest)) + widen(middle))
+    disp[...] = filled.astype(BF16)
+    gate[...] = jnp.sum(weight, axis=1, keepdims=True)
+    upper[...], lower[...] = split_parts(weight)
+    shadow = gates[ids.shape[0]:ids.shape[0] + 1, :] * mask[...].astype(F32)
+    s_weight[...] = jnp.sum(jnp.where(first == second, shadow, 0.0), axis=1, keepdims=True)
+
+
+def dispatch_kernel(tok, cot, ids, gates, mask, s_gate, s_up, s_down, out_x, out_d, out_s, out_g, upper, lower, s_weight,
+                    disp, gate, full_x, full_d, rows_x, rows_d, rows2_x, rows2_d, s_all, acc, hidden, slopes, stage, ring_send, ring_recv, own_sem,
                     a_send, a_recv, b_send, b_recv, f_send, f_recv, w_send, w_recv, pair_send, pair_recv, g_sem):
     tp, ep = lax.axis_index("tp"), lax.axis_index("ep")
     z, y, c = ep // 8, (ep // 2) % 4, ep % 2
@@ -144,6 +178,7 @@
         forward(source)
         return carry
 
+    route(ids, gates, mask, disp, gate, s_weight, upper, lower)
     for copy in local[3:]:
         copy.wait()
     select(mine, rows_x, rows_d)
@@ -161,15 +196,16 @@
             for copy in kept:
                 copy.wait()
             forward(ep)
+        if r == B_AT:
+            for copy in ring[:2]:
+                copy.wait_recv()
+            select(opposite, rows2_x, rows2_d)
+            send_rows(1, 32, rows2_x, rows2_d, opposite, b_send, b_recv)
+            kept = keep_rows(rows2_x, rows2_d, opposite, 7)
         if r >= R_START:
             lax.fori_loop(relayed, relayed + R_RATE, relay, 0)
             relayed += R_RATE
 
-    for copy in ring[:2]:
-        copy.wait_recv()
-    select(opposite, rows2_x, rows2_d)
-    send_rows(1, 32, rows2_x, rows2_d, opposite, b_send, b_recv)
-    kept = keep_rows(rows2_x, rows2_d, opposite, 7)
     for copy in ring[2:]:
         copy.wait_recv()
     lax.fori_loop(relayed, R_MID, relay, 0)
@@ -234,31 +270,32 @@
         drain(everything, f_recv.at[i])
 
 
-def dispatch_rows(tok, cot, disp, gate, s_gate, s_up, s_down, s_weight):
+def dispatch_rows(tok, cot, ids, gates, mask, s_gate, s_up, s_down):
     count, quarter = tok.shape
-    slots, part = disp.shape[0], s_gate.shape[1]
+    slots, part = 32 * SLOTS, s_gate.shape[1]
     width = 4 * quarter
     dma = pltpu.SemaphoreType.DMA
     vmem = pltpu.VMEM
     return pl.pallas_call(
         dispatch_kernel,
         out_shape=(jax.ShapeDtypeStruct((slots, width), BF16),) * 2
-        + (jax.ShapeDtypeStruct((count, width), BF16), jax.ShapeDtypeStruct((width, 3 * part), BF16)),
+        + (jax.ShapeDtypeStruct((count, width), BF16), jax.ShapeDtypeStruct((width, 3 * part), BF16))
+        + (jax.ShapeDtypeStruct((slots, count), BF16),) * 2 + (jax.ShapeDtypeStruct((count, 1), F32),),
         in_specs=[VMEM] * 8,
-        out_specs=(ANY, ANY, VMEM, ANY),
-        scratch_shapes=[vmem((count, width), BF16)] * 2 + [vmem((slots, quarter), BF16)] * 4
+        out_specs=(ANY, ANY, VMEM, ANY, VMEM, VMEM, VMEM),
+        scratch_shapes=[vmem((slots, count), BF16), vmem((slots, 1), F32)] + [vmem((count, width), BF16)] * 2 + [vmem((slots, quarter), BF16)] * 4
         + [vmem((width, 3 * part), BF16), vmem((count, 3 * part), F32), vmem((count, part), BF16),
            vmem((count, 2 * part), BF16), vmem((2, 640, 3 * part), BF16)]
         + [dma((3, 2)), dma((3, 2)), dma((9,)), dma, dma((32,)), dma, dma, dma((2,)), dma((2,)), dma((4,)), dma((4, 16)),
            dma, dma, dma((2,))],
         compiler_params=pltpu.CompilerParams(collective_id=0, has_side_effects=True),
         name="dispatch_rows",
-    )(tok, cot, disp, gate, s_gate, s_up, s_down, s_weight)
-
-
-def combine_kernel(shadow, parts, rows_x, rows_d, w_gate, w_up, w_down, back, shadow_sum, share_out, grad_gate, grad_up,
-                   grad_down, routed, all_x, all_d, down, strip_gate, strip_up, acc_gate, acc_up, acc_grad, hidden,
-                   slope_gate, slope_up, passing, relayed, far, near, total, held, pair, arrived, put_gate, put_up,
+    )(tok, cot, ids, gates, mask, s_gate, s_up, s_down)
+
+
+def combine_kernel(shadow, upper, lower, s_weight, parts, rows_x, rows_d, w_gate, w_up, w_down, mixed, share_out,
+                   grad_gate, grad_up, grad_down, back, shadow_sum, routed, all_x, all_d, down, strip, acc, acc_grad,
+                   hidden, slopes, passing, relayed, far, near, total, held, pair, arrived, put_gate, put_up,
                    put_down, pass_send, pass_recv, far_send, far_recv, near_send, near_recv, back_send,
                    back_recv, own_sem, pair_send, pair_recv, held_sem, s_send, s_recv, load_sem, put_sem):
     tp, ep = lax.axis_index("tp"), lax.axis_index("ep")
@@ -268,7 +305,7 @@
     steps = blocks + shadow.shape[0] // ROWS
     per = ROWS // SLOTS
     share = share_out.shape[0]
-    tile = strip_gate.shape[1]
+    tile, part = strip.shape[1], hidden.shape[1]
     tiles = rows_x.shape[1] // tile
     early = steps - blocks
 
@@ -297,11 +334,11 @@
                 for i, (src, dst) in enumerate(((rows_x, all_x), (rows_d, all_d), (w_down, down)))]
 
     def strips(t):
-        return [pltpu.make_async_copy(src.at[columns_of(t), :], dst.at[t % 2], load_sem.at[t, 3 + i])
-                for i, (src, dst) in enumerate(((w_gate, strip_gate), (w_up, strip_up)))]
+        return [pltpu.make_async_copy(src.at[columns_of(t), :], strip.at[t % 2, :, pl.ds(i * part, part)],
+                                      load_sem.at[t, 3 + i]) for i, src in enumerate((w_gate, w_up))]
 
     for t in range(tiles):
-        for copy in loads(t) + (strips(t) if t < 2 else []):
+        for copy in (loads(t) if t < 3 else []) + (strips(t) if t < 2 else []):
             copy.start()
 
     def take(k, carry):
@@ -368,25 +405,29 @@
         passes[i].wait_recv()
         relayed[i] = (piece(i, tp + way(i))[...].astype(F32) + passing[i].astype(F32)).astype(BF16)
         fars[i].start()
+        if i >= early:
+            nears[i].start()
 
     def ahead(t):
         for copy in loads(t) + strips(t):
             copy.wait()
-        acc_gate[...] += jnp.dot(all_x[:, columns_of(t)], strip_gate[t % 2], preferred_element_type=F32)
-        acc_up[...] += jnp.dot(all_x[:, columns_of(t)], strip_up[t % 2], preferred_element_type=F32)
+        acc[...] += jnp.dot(all_x[:, columns_of(t)], strip[t % 2], preferred_element_type=F32)
         acc_grad[...] += lax.dot_general(all_d[:, columns_of(t)], down[:, columns_of(t)], (((1,), (1,)), ((), ())),
                                          preferred_element_type=F32)
         if t + 2 < tiles:
             for copy in strips(t + 2):
                 copy.start()
+        if t + 3 < tiles:
+            for copy in loads(t + 3):
+                copy.start()
 
     def activate():
-        pre_gate, pre_up, grad = acc_gate[...], acc_up[...], acc_grad[...]
+        pre_gate, pre_up, grad = acc[:, :part], acc[:, part:], acc_grad[...]
         sigmoid = jax.nn.sigmoid(pre_gate)
         active = pre_gate * sigmoid
         hidden[...] = (active * pre_up).astype(BF16)
-        slope_gate[...] = (grad * pre_up * sigmoid * (1.0 + pre_gate * (1.0 - sigmoid))).astype(BF16)
-        slope_up[...] = (grad * active).astype(BF16)
+        slopes[:, :part] = (grad * pre_up * sigmoid * (1.0 + pre_gate * (1.0 - sigmoid))).astype(BF16)
+        slopes[:, part:] = (grad * active).astype(BF16)
 
     def project(owner):
         at = pl.ds(pl.multiple_of((owner % 4) * quarter, quarter), quarter)
@@ -403,8 +444,8 @@
         if t >= 2:
             for copy in puts(t - 2):
                 copy.wait()
-        put_gate[slot] = contract_rows(all_x[:, columns_of(t)], slope_gate[...]).astype(BF16)
-        put_up[slot] = contract_rows(all_x[:, columns_of(t)], slope_up[...]).astype(BF16)
+        both = contract_rows(all_x[:, columns_of(t)], slopes[...]).astype(BF16)
+        put_gate[slot], put_up[slot] = both[:, :part], both[:, part:]
         put_down[slot] = contract_rows(hidden[...], all_d[:, columns_of(t)]).astype(BF16)
         for copy in puts(t):
             copy.start()
@@ -455,14 +496,14 @@
         passes[i].start()
     for i in range(early):
         nears[i].start()
-    for ref in (acc_gate, acc_up, acc_grad):
+    for ref in (acc, acc_grad):
         ref[...] = jnp.zeros_like(ref)
     plan = [lambda t=t, b=b: first_leg(t, b) for t in (1, 2, 3) for b in (1, 2, 3, 0)]
     plan = plan[:10] + [lambda: second_leg(1), plan[10], lambda: second_leg(2), plan[11], lambda: second_leg(3)]
     for t in range(tiles):
-        if 1 <= t <= 4:
-            lax.fori_loop(4 * t - 4, 4 * t, join, 0)
-        if t == 5:
+        if t >= 2:
+            lax.fori_loop(2 * t - 4, 2 * t - 2, join, 0)
+        if t == tiles - 1:
             for b in (1, 2, 3, 0):
                 for q in range(4):
                     hand_on(q, 1, b, True, b)
@@ -477,8 +518,6 @@
         passes[i].start()
     project(tp + 1)
     project(tp + 3)
-    for i in range(early, steps):
-        nears[i].start()
     project(tp)
     for i in range(early):
         finish(i)
@@ -508,20 +547,24 @@
         drain(parts.at[pl.ds(0, 15 * (CUTS[q + 1] - CUTS[q])), :], s_send.at[q])
     drain(back.at[pl.ds(0, 31 * SLOTS), :], back_send)
     drain(back.at[pl.ds(0, 31 * SLOTS), :], back_recv)
-
-
-def combine_rows(shadow, parts, rows_x, rows_d, w_gate, w_up, w_down):
+    result = contract_rows(upper[...], back[...]) + contract_rows(lower[...], back[...])
+    mixed[...] = (result + s_weight[...] * shadow_sum[...]).astype(BF16)
+
+
+def combine_rows(shadow, upper, lower, s_weight, parts, rows_x, rows_d, w_gate, w_up, w_down):
     (slots, width), (count, _) = rows_x.shape, shadow.shape
     quarter, part, share, steps, tile = width // 4, w_gate.shape[1], width // 32, (slots + count) // ROWS, 512
     dma, vmem, like = pltpu.SemaphoreType.DMA, pltpu.VMEM, jax.ShapeDtypeStruct
     return pl.pallas_call(
         combine_kernel,
-        out_shape=(like((slots, quarter), BF16), like((count, quarter), F32), like((share, 3 * part), BF16),
+        out_shape=(like((count, quarter), BF16), like((share, 3 * part), BF16),
                    like((width, part), BF16), like((width, part), BF16), like((part, width), BF16)),
-        in_specs=[VMEM] + [ANY] * 6,
-        out_specs=(VMEM, VMEM, VMEM, ANY, ANY, ANY),
-        scratch_shapes=[vmem((slots, width), BF16)] * 3 + [vmem((part, width), BF16)] + [vmem((2, tile, part), BF16)] * 2
-        + [vmem((slots, part), F32)] * 3 + [vmem((slots, part), BF16)] * 3
+        in_specs=[VMEM] * 4 + [ANY] * 6,
+        out_specs=(VMEM, VMEM, ANY, ANY, ANY),
+        scratch_shapes=[vmem((slots, quarter), BF16), vmem((count, quarter), F32)]
+        + [vmem((slots, width), BF16)] * 3 + [vmem((part, width), BF16), vmem((2, tile, 2 * part), BF16)]
+        + [vmem((slots, 2 * part), F32), vmem((slots, part), F32), vmem((slots, part), BF16),
+           vmem((slots, 2 * part), BF16)]
         + [vmem((steps, ROWS, quarter), BF16)] * 4 + [vmem((slots // ROWS, ROWS, quarter), BF16)]
         + [vmem((16, share, 3 * part), BF16)] * 2 + [vmem((15, share, 3 * part), BF16)]
         + [vmem((2, tile, part), BF16)] * 2 + [vmem((2, part, tile), BF16)]
@@ -529,39 +572,21 @@
         + [dma, dma((16,)), dma((16,)), dma((4,)), dma((4, 15)), dma((width // tile, 5)), dma((2, 3))],
         compiler_params=pltpu.CompilerParams(collective_id=1, has_side_effects=True, vmem_limit_bytes=VMEM_BYTES),
         name="combine_rows",
-    )(shadow, parts, rows_x, rows_d, w_gate, w_up, w_down)
+    )(shadow, upper, lower, s_weight, parts, rows_x, rows_d, w_gate, w_up, w_down)
 
 
 def shards(tokens, cotangent, expert_ids, gate_weights, shadow_mask, w_gate, w_up, w_down, s_gate, s_up, s_down):
-    tok_count, top_count = expert_ids.shape
-    quarter = tokens.shape[1]
-    width = 4 * quarter
-    experts = 32
-    slot_count = experts * SLOTS
-    picks = expert_ids.reshape(-1)
-    onehot = (picks[:, None] == jnp.arange(experts, dtype=jnp.int32)[None, :]).astype(jnp.int32)
-    rank = jnp.sum((jnp.cumsum(onehot, axis=0) - onehot) * onehot, axis=1)
-    slot_index = (picks * SLOTS + rank).reshape(tok_count, top_count)
-    matches = jnp.arange(slot_count, dtype=jnp.int32)[:, None, None] == slot_index[None, :, :]
-    dispatch = jnp.any(matches, axis=2).astype(BF16)
-    weighting = jnp.sum(jnp.where(matches, gate_weights[None, :, :top_count], 0.0), axis=2)
-    slot_gate = jnp.sum(weighting, axis=1, keepdims=True)
-    shadow_weight = gate_weights[:, top_count] * shadow_mask.astype(F32)
-
-    expert_x, expert_d, shadow_out, shadow_part = dispatch_rows(
-        tokens, cotangent, dispatch, slot_gate, s_gate, s_up, s_down.T, shadow_weight[:, None])
+    expert_x, expert_d, shadow_out, shadow_part, upper, lower, s_weight = dispatch_rows(
+        tokens, cotangent, expert_ids.T, gate_weights.T, shadow_mask[None, :], s_gate, s_up, s_down.T)
     part = s_gate.shape[1]
 
-    back, shadow_sum, shadow_sums, grad_gate, grad_up, grad_down = combine_rows(
-        shadow_out, shadow_part, expert_x, expert_d, w_gate[0], w_up[0], w_down[0])
+    mixed, shadow_sums, grad_gate, grad_up, grad_down = combine_rows(
+        shadow_out, upper, lower, s_weight, shadow_part, expert_x, expert_d, w_gate[0], w_up[0], w_down[0])
     grad_gate, grad_up, grad_down = grad_gate[None], grad_up[None], grad_down[None]
     grad_s_gate = shadow_sums[:, :part]
     grad_s_up = shadow_sums[:, part:2 * part]
     grad_s_down = shadow_sums[:, 2 * part:].T
 
-    upper, lower = split_parts(weighting.T)
-    combined = jnp.dot(upper, back, preferred_element_type=F32) + jnp.dot(lower, back, preferred_element_type=F32)
-    mixed = (combined + shadow_weight[:, None] * shadow_sum).astype(BF16)
     return mixed, grad_gate, grad_up, grad_down, grad_s_gate, grad_s_up, grad_s_down
 
 

time: 221 us -> 198 us (0.90)
  Pallas kernels: 197 us -> 184 us
  matrix products: 4.26 us -> 0 us
  other arithmetic: 4.08 us -> 0 us
    pallas_call x1, Pallas kernels: 85.4 us -> 77.6 us  [combine_rows(): pl.pallas_call(combine_kernel, out_shape=(like((count, quarter), BF16), l...]
    pallas_call x1, Pallas kernels: 112 us -> 106 us  [dispatch_rows(): pl.pallas_call(dispatch_kernel, out_shape=(jax.ShapeDtypeStruct((slots, w...]
    dot_general x2 -> x0, matrix products: 4.26 us -> none  [the longest x1 2.58 us: shards(): jnp.dot(lower, back, preferred_element_type=F32)]
    unnamed x10 -> x8, local copies, waits for them, and re-layouts: 9.78 us -> 11.8 us
where the time goes in v3:
time: 198 us
  Pallas kernels  184 us (93%)
  local copies, waits for them, and re-layouts  13.5 us (7%)
    pallas_call x1, Pallas kernels, dispatch_rows(): pl.pallas_call(dispatch_kernel, out_shape=(jax.ShapeDtypeStruct((slots, w...  106 us
    pallas_call x1, Pallas kernels, combine_rows(): pl.pallas_call(combine_kernel, out_shape=(like((count, quarter), BF16), l...  77.6 us
    unnamed x8, local copies, waits for them, and re-layouts  11.8 us

profile of v3, /device:TPU:1, one launch (start us, length us, event | category | flops | bytes accessed | tf_op | source)
XLA Modules:
  0.0 197.8 jit_solution(15177242993684792109)
XLA Ops:
  0.6 106.0 %dispatch_rows.1 = (bf16[512,5120]{1,0:T(8,128)(2,1)}, bf16[512,5120]{1,0:T(8,128)(2,1)}, bf16[128,5120]{1,0:T(8,128)(2,1)}, bf16[5120,1152]{1,0:T(8,128)(2,1)},...) custom-call(bf16[128,1280]{1,0:T(8,128)(2,1)} %tok.1, bf16[128,1280]{1,0:T(8,128)(2,1)} %cot.1, ...), custom_call_target="tpu_custom_call" | custom-call | tf_op jit(solution)/shard_map/dispatch_rows/pallas_call | solution.py:279
  106.7 77.6 %combine_rows.1 = (bf16[128,1280]{1,0:T(8,128)(2,1)}, bf16[160,1152]{1,0:T(8,128)(2,1)}, bf16[5120,384]{1,0:T(8,128)(2,1)}, bf16[5120,384]{1,0:T(8,128)(2,1)}, bf16[384,5120]{1,0:T(8,128)(2,1)}) custom-call(bf16[128,5120]{1,0:T(8,128)(2,1)} %get-tuple-element.19.shadow, bf16[512,128]{1,0:T(8,128)(2,1)} %get-tuple-element.20.upper, ...), custom_call_target="tpu_custom_call" | custom-call | tf_op jit(solution)/shard_map/combine_rows/pallas_call | solution.py:558
  184.3 1.8 slice_bitcast_fusion
  186.0 1.7 copy.22
  187.7 0.0 copy-start.1
  187.7 4.6 %copy.23 = bf16[1,5120,384]{2,1,0:T(8,128)(2,1)} copy(bf16[1,5120,384]{2,1,0:T(8,128)(2,1)} %bitcast.17) | data formatting | bytes 7864320
  192.3 0.0 copy-done.1
  192.3 0.0 copy-start
  192.3 2.0 %copy.24 = bf16[1,5120,384]{2,1,0:T(8,128)(2,1)} copy(bf16[1,5120,384]{2,1,0:T(8,128)(2,1)S(1)} %bitcast.16) | data formatting | bytes 7864320
  194.3 1.5 copy-done
  195.9 1.9 copy.25
Async XLA Ops:
  187.7 4.6 %copy-start.1 = (bf16[5120,384]{1,0:T(8,128)(2,1)S(1)}, bf16[5120,384]{1,0:T(8,128)(2,1)}, u32[]{:S(2)}) copy-start(bf16[5120,384]{1,0:T(8,128)(2,1)} %get-tuple-element.28) | copy-start | bytes 11796484
  192.3 3.5 %copy-start = (bf16[384,5120]{1,0:T(8,128)(2,1)S(1)}, bf16[384,5120]{1,0:T(8,128)(2,1)}, u32[]{:S(2)}) copy-start(bf16[384,5120]{1,0:T(8,128)(2,1)} %get-tuple-element.29) | copy-start | bytes 11796484

commit v4 on v3

--- a/solution.py
+++ b/solution.py
@@ -575,6 +575,23 @@
     )(shadow, upper, lower, s_weight, parts, rows_x, rows_d, w_gate, w_up, w_down)
 
 
+def settle_kernel(*refs):
+    for src, dst in zip(refs[:4], refs[4:]):
+        dst[...] = src[...]
+
+
+def settle(mixed, grad_gate, grad_up, grad_down):
+    (count, quarter), (width, part) = mixed.shape, grad_gate.shape
+    steps = 5
+    tall = pl.BlockSpec((width // steps, part), lambda i: (i, 0))
+    specs = [pl.BlockSpec((count, quarter // steps), lambda i: (0, i)), tall, tall,
+             pl.BlockSpec((part, width // steps), lambda i: (0, i))]
+    arrays = (mixed, grad_gate, grad_up, grad_down)
+    return pl.pallas_call(
+        settle_kernel, grid=(steps,), out_shape=tuple(jax.ShapeDtypeStruct(a.shape, a.dtype) for a in arrays),
+        in_specs=specs, out_specs=tuple(specs), name="settle")(*arrays)
+
+
 def shards(tokens, cotangent, expert_ids, gate_weights, shadow_mask, w_gate, w_up, w_down, s_gate, s_up, s_down):
     expert_x, expert_d, shadow_out, shadow_part, upper, lower, s_weight = dispatch_rows(
         tokens, cotangent, expert_ids.T, gate_weights.T, shadow_mask[None, :], s_gate, s_up, s_down.T)
@@ -582,6 +599,7 @@
 
     mixed, shadow_sums, grad_gate, grad_up, grad_down = combine_rows(
         shadow_out, upper, lower, s_weight, shadow_part, expert_x, expert_d, w_gate[0], w_up[0], w_down[0])
+    mixed, grad_gate, grad_up, grad_down = settle(mixed, grad_gate, grad_up, grad_down)
     grad_gate, grad_up, grad_down = grad_gate[None], grad_up[None], grad_down[None]
     grad_s_gate = shadow_sums[:, :part]
     grad_s_up = shadow_sums[:, part:2 * part]

time: 198 us -> 196 us (0.990)
  local copies, waits for them, and re-layouts: 13.5 us -> 0.75 us
  Pallas kernels: 184 us -> 194 us
    unnamed x8 -> x2, local copies, waits for them, and re-layouts: 11.8 us -> 0.01 us
    pallas_call x0 -> x1, Pallas kernels: none -> 10.7 us  [settle(): pl.pallas_call(settle_kernel, grid=(steps,), out_shape=tuple((jax.ShapeDt...]
where the time goes in v4:
time: 196 us
  Pallas kernels  194 us (99%)
    pallas_call x1, Pallas kernels, dispatch_rows(): pl.pallas_call(dispatch_kernel, out_shape=(jax.ShapeDtypeStruct((slots, w...  106 us
    pallas_call x1, Pallas kernels, combine_rows(): pl.pallas_call(combine_kernel, out_shape=(like((count, quarter), BF16), l...  77.6 us
    pallas_call x1, Pallas kernels, settle(): pl.pallas_call(settle_kernel, grid=(steps,), out_shape=tuple((jax.ShapeDt...  10.7 us

profile of v4, /device:TPU:1, one launch (start us, length us, event | category | flops | bytes accessed | tf_op | source)
XLA Modules:
  0.0 195.7 jit_solution(5458408993032330707)
XLA Ops:
  0.6 106.0 %dispatch_rows.1 = (bf16[512,5120]{1,0:T(8,128)(2,1)}, bf16[512,5120]{1,0:T(8,128)(2,1)}, bf16[128,5120]{1,0:T(8,128)(2,1)}, bf16[5120,1152]{1,0:T(8,128)(2,1)},...) custom-call(bf16[128,1280]{1,0:T(8,128)(2,1)} %tok.1, bf16[128,1280]{1,0:T(8,128)(2,1)} %cot.1, ...), custom_call_target="tpu_custom_call" | custom-call | tf_op jit(solution)/shard_map/dispatch_rows/pallas_call | solution.py:279
  106.7 77.6 %combine_rows.1 = (bf16[128,1280]{1,0:T(8,128)(2,1)}, bf16[160,1152]{1,0:T(8,128)(2,1)}, bf16[5120,384]{1,0:T(8,128)(2,1)}, bf16[5120,384]{1,0:T(8,128)(2,1)}, bf16[384,5120]{1,0:T(8,128)(2,1)}) custom-call(bf16[128,5120]{1,0:T(8,128)(2,1)} %get-tuple-element.23.shadow, bf16[512,128]{1,0:T(8,128)(2,1)} %get-tuple-element.24.upper, ...), custom_call_target="tpu_custom_call" | custom-call | tf_op jit(solution)/shard_map/combine_rows/pallas_call | solution.py:558
  184.3 0.0 copy-start
  184.3 10.7 %settle.1 = (bf16[128,1280]{1,0:T(8,128)(2,1)}, bf16[5120,384]{1,0:T(8,128)(2,1)}, bf16[5120,384]{1,0:T(8,128)(2,1)}, bf16[384,5120]{1,0:T(8,128)(2,1)}) custom-call(bf16[128,1280]{1,0:T(8,128)(2,1)} %get-tuple-element.30.refs_0_, bf16[5120,384]{1,0:T(8,128)(2,1)} %get-tuple-element.31.refs_1_, bf16[5120,384]{1,0:T(8,128)(2,1)} %get-tuple-element.32.refs_2_, ...), custom_call_target="tpu_custom_call" | custom-call | tf_op jit(solution)/shard_map/settle/pallas_call | solution.py:590
  195.0 0.0 copy-done
  195.0 0.7 slice_bitcast_fusion
Async XLA Ops:
  184.3 10.7 %copy-start = (bf16[160,1152]{1,0:T(8,128)(2,1)S(1)}, bf16[160,1152]{1,0:T(8,128)(2,1)}, u32[]{:S(2)}) copy-start(bf16[160,1152]{1,0:T(8,128)(2,1)} %get-tuple-element.38) | copy-start | bytes 1105924
